TPU v7x, 32 devices: a whole 2x2x4 slice. The times are simulated.
32 devices in a mesh: src: 4 (over y, x), tgt: 8 (over z, core).
Axes of the slice: x: 2, y: 2, z: 4, core: 2. Of those that a mesh axis runs over, the one named last changes fastest.
Arguments:
- source_pca: float32 [64, 16384], P(None, 'src'), may hold values from -6 to 6
- target_pca: float32 [64, 8192], P(None, 'tgt'), may hold values from -6 to 6
- source_labels: int32 [16384], P('src'), may hold values from 0 to 63, as said below
- target_labels: int32 [8192], P('tgt'), may hold values from 0 to 63, as said below
- block_mask: int32 [64, 64], replicated, may hold values from 0 to 1, as said below
Outputs:
- source_projection: float32 [64, 16384], P(None, ('src', 'tgt'))
- target_projection: float32 [64, 8192], P(None, 'tgt')
Inputs may be any that keep to these rules, and one draw needn't show every extreme that they name: `source_labels`: each aligned block of 4096 consecutive source cells holds every one of the 64 clusters. `target_labels`: each aligned block of 1024 consecutive target cells holds every one of the 64 clusters. `block_mask`: entries are 0 or 1, and the diagonal is all ones.
All inputs are finite; a program needn't handle non-finite values.
Results may differ from a plain program's by a relative error of at most 0.0003.
Values sent between devices are 32-bit elements; how exact they have to be, the bound alone decides.
No kernel may reach another device: no remote copies, remote signals or barrier semaphores. Data moves between devices by JAX's collectives and lax.ppermute only.
A program may use at most 64 MiB of HBM per device.

v0:
```python
import math

import jax
import jax.numpy as jnp
from jax import lax
from jax.sharding import PartitionSpec as P

ITERS = 2


EPSILON = 0.05
FLOOR = -1e30


def combined_all(value, axis, combine):
    everything = jax.tree.map(lambda part: lax.all_gather(part, axis), value)
    initial = jax.tree.map(lambda part: part[0], everything)

    def step(k, so_far):
        return combine(so_far, jax.tree.map(lambda part: part[k], everything))

    return lax.fori_loop(1, lax.axis_size(axis), step, initial)


def combine_pair(first, second):
    top = jnp.maximum(first[0], second[0])
    return (top, first[1] * jnp.exp(first[0] - top) + second[1] * jnp.exp(second[0] - top))


def shards(source_pca, target_pca, source_labels, target_labels, block_mask):
    dims, rows = source_pca.shape
    cols = target_pca.shape[1]
    clusters = block_mask.shape[0]
    total_rows = rows * lax.axis_size("src")
    total_cols = cols * lax.axis_size("tgt")
    rblock = min(512, rows)
    nblock = rows // rblock
    xblocks = source_pca.reshape(dims, nblock, rblock).transpose(1, 0, 2)
    xsquare = jnp.sum(source_pca * source_pca, 0).reshape(nblock, rblock)
    ysquare = jnp.sum(target_pca * target_pca, 0)
    series = jnp.arange(clusters, dtype=jnp.int32)
    source_onehot = (source_labels[:, None] == series[None, :]).astype(jnp.float32)
    target_onehot = (target_labels[:, None] == series[None, :]).astype(jnp.float32)
    allowed = jnp.dot(
        source_onehot, block_mask.astype(jnp.float32), precision=lax.Precision.HIGHEST
    )
    reach = (
        lax.dot_general(
            allowed, target_onehot, (((1,), (1,)), ((), ())), precision=lax.Precision.HIGHEST
        )
        > 0.5
    )
    reach_blocks = reach.reshape(nblock, rblock, cols)

    def logits(xb, xsq, act, shift_rows, shift_cols):
        cross = lax.dot_general(
            xb, target_pca, (((0,), (0,)), ((), ())), precision=lax.Precision.HIGHEST
        )
        cost = (xsq[:, None] + ysquare[None, :] - 2.0 * cross) / dims
        return jnp.where(
            act, (shift_rows[:, None] + shift_cols[None, :] - cost) / EPSILON, -jnp.inf
        )

    zero_rows = jnp.zeros((rblock,), jnp.float32)
    zero_cols = jnp.zeros((cols,), jnp.float32)

    def row_update(g_pot):

        def one_block(item):
            xb, xsq, act = item
            z = logits(xb, xsq, act, zero_rows, g_pot)
            peak = jnp.max(z, 1)
            return (peak, jnp.sum(jnp.exp(z - peak[:, None]), 1))

        peak, total = lax.map(one_block, (xblocks, xsquare, reach_blocks))
        peak = peak.reshape(rows)
        total = total.reshape(rows)
        peak, total = combined_all((peak, total), "tgt", combine_pair)
        return -EPSILON * math.log(total_rows) - EPSILON * (peak + jnp.log(total))

    def col_update(f_pot):

        def col_step(carry, item):
            peak, total = carry
            xb, xsq, act, fb = item
            z = logits(xb, xsq, act, fb, zero_cols)
            newer = jnp.maximum(peak, jnp.max(z, 0))
            total = total * jnp.exp(peak - newer) + jnp.sum(jnp.exp(z - newer[None, :]), 0)
            return ((newer, total), None)

        init = (jnp.full((cols,), FLOOR, jnp.float32), jnp.zeros((cols,), jnp.float32))
        fblocks = f_pot.reshape(nblock, rblock)
        (peak, total), unused = lax.scan(col_step, init, (xblocks, xsquare, reach_blocks, fblocks))
        peak, total = combined_all((peak, total), "src", combine_pair)
        return -EPSILON * math.log(total_cols) - EPSILON * (peak + jnp.log(total))

    g_pot = jnp.zeros((cols,), jnp.float32)
    f_pot = jnp.zeros((rows,), jnp.float32)
    for step in range(ITERS):
        f_pot = row_update(g_pot)
        g_pot = col_update(f_pot)

    def proj_step(carry, item):
        peak, total, weighted = carry
        xb, xsq, act, fb = item
        z = logits(xb, xsq, act, fb, g_pot)
        rpeak = jnp.max(z, 1)
        rprob = jnp.exp(z - rpeak[:, None])
        rweight = lax.dot_general(
            target_pca, rprob, (((1,), (1,)), ((), ())), precision=lax.Precision.HIGHEST
        )
        newer = jnp.maximum(peak, jnp.max(z, 0))
        cprob = jnp.exp(z - newer[None, :])
        scale = jnp.exp(peak - newer)
        total = total * scale + jnp.sum(cprob, 0)
        weighted = weighted * scale[None, :] + jnp.dot(xb, cprob, precision=lax.Precision.HIGHEST)
        return ((newer, total, weighted), (rpeak, jnp.sum(rprob, 1), rweight))

    init = (
        jnp.full((cols,), FLOOR, jnp.float32),
        jnp.zeros((cols,), jnp.float32),
        jnp.zeros((dims, cols), jnp.float32),
    )
    fblocks = f_pot.reshape(nblock, rblock)
    (cpeak, ctotal, cweighted), (rpeak, rmass, rweight) = lax.scan(
        proj_step, init, (xblocks, xsquare, reach_blocks, fblocks)
    )
    rpeak = rpeak.reshape(rows)
    rmass = rmass.reshape(rows)
    rweight = rweight.transpose(1, 0, 2).reshape(dims, rows)
    top = lax.pmax(rpeak, "tgt")
    factor = jnp.exp(rpeak - top)
    mass_all, weight_all = lax.psum((rmass * factor, rweight * factor[None, :]), "tgt")
    share = rows // lax.axis_size("tgt")
    start = lax.axis_index("tgt") * share
    mass_part = lax.dynamic_slice_in_dim(mass_all, start, share, 0)
    weight_part = lax.dynamic_slice_in_dim(weight_all, start, share, 1)
    source_projection = weight_part / mass_part[None, :]
    ctop = lax.pmax(cpeak, "src")
    cfactor = jnp.exp(cpeak - ctop)
    csum, cweight = lax.psum((ctotal * cfactor, cweighted * cfactor[None, :]), "src")
    target_projection = cweight / csum[None, :]
    return (source_projection, target_projection)


def solution(mesh):
    placed = (P(None, "src"), P(None, "tgt"), P("src"), P("tgt"), P())
    return jax.shard_map(
        shards,
        mesh=mesh,
        in_specs=placed,
        out_specs=(P(None, ("src", "tgt")), P(None, "tgt")),
        check_vma=False,
    )
```

profile of v0, /device:TPU:0, one launch (start us, length us, event | category | flops | bytes accessed | tf_op | source)
XLA Modules:
  0.0 453.7 jit_solution(11823418697811945413)
XLA Ops:
  13.6 10.3 %broadcast_compare_fusion = pred[4096,1024]{1,0:T(32,128)(4,1)} fusion(f32[4096,64]{0,1:T(8,128)S(1)} %fusion.30, s32[1024]{0:T(1024)S(1)} %copy-done.4), kind=kOutput, calls=%fused_computation.69 | convolution fusion | flops 3225485312 | bytes 5246976 | tf_op jit(solution)/shard_map/dot_general | solution.py:48
  23.9 34.4 %while.139 = (s32[]{:T(128)}, f32[8,512]{1,0:T(8,128)S(1)}, f32[8,512]{1,0:T(8,128)S(1)}, pred[8,512,1024]{2,1,0:T(32,128)(4,1)}, f32[8,512]{1,0:T(8,128)S(1)}, ...) while((s32[]{:T(128)}, f32[8,512]{1,0:T(8,128)S(1)}, ...), condition=%wide.region_5.6_spmd, body=%wide.region_2.5_spmd.sunk | while | flops 407895040 | bytes 5137529 | solution.py:75
  23.9 3.7 fusion.67
  28.2 3.7 fusion.67
  32.5 3.7 fusion.67
  36.8 3.7 fusion.67
  41.2 3.7 fusion.67
  45.5 3.7 fusion.67
  49.8 3.7 fusion.67
  54.1 3.7 fusion.67
  58.4 15.7 %all-gather.4 = f32[8,1,4096]{2,1,0:T(1,128)S(1)} all-gather(f32[1,1,4096]{2,1,0:T(1,128)S(1)} %reshape.85), channel_id=1, replica_groups=mesh['src'=4,'tgt'=8] {'tgt'}, dimensions={0}, use_global_device_ids=true | all-gather | bytes 147456 | tf_op jit(solution)/shard_map/all_gather | solution.py:16
  74.2 14.2 %all-gather.5 = f32[8,1,4096]{2,1,0:T(1,128)S(1)} all-gather(f32[1,1,4096]{2,1,0:T(1,128)S(1)} %reshape.87), channel_id=1, replica_groups=mesh['src'=4,'tgt'=8] {'tgt'}, dimensions={0}, use_global_device_ids=true | all-gather | bytes 147456 | tf_op jit(solution)/shard_map/all_gather | solution.py:16
  89.1 31.9 %while.145 = (s32[]{:T(128)}, f32[1024]{0:T(1024)S(1)}, f32[1024]{0:T(1024)S(1)}, pred[8,512,1024]{2,1,0:T(32,128)(4,1)}, f32[8,512]{1,0:T(8,128)S(1)}, /*index=...) while((s32[]{:T(128)}, f32[1024]{0:T(1024)S(1)}, ...), condition=%wide.region_11.12_spmd.clone, body=%wide.region_8.11_spmd.clone.sunk | while | flops 407901184 | bytes 5182596 | solution.py:93
  89.1 3.6 fusion.71
  93.1 3.6 fusion.71
  97.1 3.6 fusion.71
  101.1 3.6 fusion.71
  105.1 3.6 fusion.71
  109.1 3.6 fusion.71
  113.1 3.6 fusion.71
  117.0 3.6 fusion.71
  121.0 8.2 %all-gather = f32[4096]{0:T(1024)S(1)} all-gather(f32[1024]{0:T(1024)S(1)} %get-tuple-element.802), channel_id=2, replica_groups=mesh['src'=4,'tgt'=8] {'src'}, dimensions={0}, use_global_device_ids=true | all-gather | bytes 20480 | tf_op jit(solution)/shard_map/all_gather | solution.py:16
  129.2 8.2 %all-gather.1 = f32[4096]{0:T(1024)S(1)} all-gather(f32[1024]{0:T(1024)S(1)} %get-tuple-element.803), channel_id=3, replica_groups=mesh['src'=4,'tgt'=8] {'src'}, dimensions={0}, use_global_device_ids=true | all-gather | bytes 20480 | tf_op jit(solution)/shard_map/all_gather | solution.py:16
  137.6 34.6 %while.142 = (s32[]{:T(128)}, f32[8,512]{1,0:T(8,128)S(1)}, f32[8,512]{1,0:T(8,128)S(1)}, pred[8,512,1024]{2,1,0:T(32,128)(4,1)}, f32[1024]{0:T(1024)S(1)}, /*in...) while((s32[]{:T(128)}, f32[8,512]{1,0:T(8,128)S(1)}, ...), condition=%wide.region_17.18_spmd, body=%wide.region_14.17_spmd.sunk | while | flops 407895040 | bytes 5141633 | solution.py:75
  137.6 3.7 fusion.69
  142.0 3.7 fusion.69
  146.3 3.7 fusion.69
  150.6 3.7 fusion.69
  154.9 3.7 fusion.69
  159.2 3.7 fusion.69
  163.6 3.7 fusion.69
  167.9 3.7 fusion.69
  172.2 14.0 %all-gather.6 = f32[8,1,4096]{2,1,0:T(1,128)S(1)} all-gather(f32[1,1,4096]{2,1,0:T(1,128)S(1)} %reshape.89), channel_id=1, replica_groups=mesh['src'=4,'tgt'=8] {'tgt'}, dimensions={0}, use_global_device_ids=true | all-gather | bytes 147456 | tf_op jit(solution)/shard_map/all_gather | solution.py:16
  186.3 14.0 %all-gather.7 = f32[8,1,4096]{2,1,0:T(1,128)S(1)} all-gather(f32[1,1,4096]{2,1,0:T(1,128)S(1)} %reshape.91), channel_id=1, replica_groups=mesh['src'=4,'tgt'=8] {'tgt'}, dimensions={0}, use_global_device_ids=true | all-gather | bytes 147456 | tf_op jit(solution)/shard_map/all_gather | solution.py:16
  201.1 31.9 %while.146 = (s32[]{:T(128)}, f32[1024]{0:T(1024)S(1)}, f32[1024]{0:T(1024)S(1)}, pred[8,512,1024]{2,1,0:T(32,128)(4,1)}, f32[8,512]{1,0:T(8,128)S(1)}, /*index=...) while((s32[]{:T(128)}, f32[1024]{0:T(1024)S(1)}, ...), condition=%wide.region_23.24_spmd.clone, body=%wide.region_20.23_spmd.clone.sunk | while | flops 407901184 | bytes 5182596 | solution.py:93
  201.1 3.6 fusion.74
  205.1 3.6 fusion.74
  209.1 3.6 fusion.74
  213.1 3.6 fusion.74
  217.1 3.6 fusion.74
  221.1 3.6 fusion.74
  225.1 3.6 fusion.74
  229.1 3.6 fusion.74
  233.0 7.2 %all-gather.2 = f32[4096]{0:T(1024)S(1)} all-gather(f32[1024]{0:T(1024)S(1)} %get-tuple-element.810), channel_id=4, replica_groups=mesh['src'=4,'tgt'=8] {'src'}, dimensions={0}, use_global_device_ids=true | all-gather | bytes 20480 | tf_op jit(solution)/shard_map/all_gather | solution.py:16
  240.3 8.4 %all-gather.3 = f32[4096]{0:T(1024)S(1)} all-gather(f32[1024]{0:T(1024)S(1)} %get-tuple-element.811), channel_id=5, replica_groups=mesh['src'=4,'tgt'=8] {'src'}, dimensions={0}, use_global_device_ids=true | all-gather | bytes 20480 | tf_op jit(solution)/shard_map/all_gather | solution.py:16
  248.9 82.9 %while.147 = (s32[]{:T(128)}, f32[1024]{0:T(1024)S(1)}, f32[1024]{0:T(1024)S(1)}, f32[64,1024]{1,0:T(8,128)S(1)}, f32[8,512]{1,0:T(8,128)S(1)}, /*index=5*/f32[8...) while((s32[]{:T(128)}, f32[1024]{0:T(1024)S(1)}, ...), condition=%wide.region_31.32_spmd.clone, body=%wide.region_26.31_spmd.clone.sunk | while | flops 1216548864 | bytes 10458301 | solution.py:125
  248.9 3.9 fusion.79
  259.3 3.9 fusion.79
  269.6 3.9 fusion.79
  276.9 3.1 fusion.83
  280.0 3.9 fusion.79
  287.3 3.1 fusion.83
  290.3 3.9 fusion.79
  297.6 3.1 fusion.83
  300.7 3.9 fusion.79
  311.1 3.9 fusion.79
  318.4 3.1 fusion.83
  321.4 3.9 fusion.79
  328.7 3.1 fusion.83
  331.8 8.9 %pmax.15 = f32[1024]{0:T(1024)S(1)} all-reduce(f32[1024]{0:T(1024)S(1)} %get-tuple-element.818), channel_id=1, replica_groups=mesh['src'=4,'tgt'=8] {'src'}, use_global_device_ids=true, to_apply=%region_35.36 | all-reduce | flops 1024 | bytes 8192 | tf_op jit(solution)/shard_map/pmax | solution.py:139
  342.8 25.9 %pmax.14 = f32[4096]{0:T(1024)S(1)} all-reduce(f32[4096]{0:T(1024)S(1)} %bitcast.196), channel_id=1, replica_groups=mesh['src'=4,'tgt'=8] {'tgt'}, use_global_device_ids=true, to_apply=%region_32.33 | all-reduce | flops 4096 | bytes 32768 | tf_op jit(solution)/shard_map/pmax | solution.py:131
  369.9 25.9 %psum.29 = f32[4096]{0:T(1024)S(1)} all-reduce(f32[4096]{0:T(1024)S(1)} %get-tuple-element.1177), channel_id=1, replica_groups=mesh['src'=4,'tgt'=8] {'tgt'}, use_global_device_ids=true, to_apply=%region_34.35 | all-reduce | flops 4096 | bytes 32768 | tf_op jit(solution)/shard_map/psum | solution.py:133
  395.9 8.1 %psum.31 = f32[1024]{0:T(1024)S(1)} all-reduce(f32[1024]{0:T(1024)S(1)} %get-tuple-element.1175), channel_id=1, replica_groups=mesh['src'=4,'tgt'=8] {'src'}, use_global_device_ids=true, to_apply=%region_37.38 | all-reduce | flops 1024 | bytes 8192 | tf_op jit(solution)/shard_map/psum | solution.py:141
  405.7 39.6 %all-reduce.3.cloned.1.call-done = f32[64,4096]{1,0:T(8,128)} async-done(((f32[64,4096]{1,0:T(8,128)}), f32[64,4096]{1,0:T(8,128)}) %all-reduce.3.cloned.1.call-update) | async-done | bytes 1048592 | tf_op jit(solution)/shard_map/psum | solution.py:133
  (326 shorter events, 67.3 us)
Async XLA Ops:
  7.2 2.5 copy-start.1
  7.2 396.8 %all-reduce.5.cloned.1.call-start = ((), (), s32[]{:S(2)}) async-start(), calls=%async_computation.1 | async-start | bytes 524288 | tf_op jit(solution)/shard_map/psum | solution.py:141
  9.7 2.3 copy-start.2
  9.7 2.3 copy-start.3
  10.3 3.3 copy-start.4
  13.6 10.3 %copy-start = (f32[64,1024]{1,0:T(8,128)S(1)}, f32[64,1024]{1,0:T(8,128)}, u32[]{:S(2)}) copy-start(f32[64,1024]{1,0:T(8,128)} %param.24) | copy-start | bytes 786436
  341.4 103.9 %all-reduce.3.cloned.1.call-start = ((), (), s32[]{:S(2)}) async-start(), calls=%async_computation | async-start | bytes 2097152 | tf_op jit(solution)/shard_map/psum | solution.py:133
Sparse Core Ops, SparseCore 0:
  341.6 42.0 all-reduce.4
  386.0 59.2 all-reduce.2
where the time goes:
time: 455 us; the launch traced here: 454 us
  matrix products  203 us (45%)
  blocking collectives  159 us (35%)
  waiting for transfers between devices  39.7 us (9%)
  other arithmetic  27.1 us (6%)
  between operations  14.4 us (3%)
  local copies, waits for them, and re-layouts  7.89 us (2%)
    dot_general x40, matrix products, logits(): lax.dot_general(xb, target_pca, (((0,), (0,)), ((), ())), precision=lax.P...  147 us
    all_gather x8, blocking collectives, combined_all(): everything = jax.tree.map(lambda part: lax.all_gather(part, axis), value)  89.9 us
    psum x1, waiting for transfers between devices, shards(): lax.psum((rmass * factor, rweight * factor[None, :]), 'tgt')  39.6 us
    psum x1, blocking collectives, shards(): lax.psum((rmass * factor, rweight * factor[None, :]), 'tgt')  25.9 us
    pmax x1, blocking collectives, shards(): top = lax.pmax(rpeak, 'tgt')  25.9 us
    dot_general x8, matrix products, proj_step(): lax.dot_general(target_pca, rprob, (((1,), (1,)), ((), ())), precision=la...  24.5 us
    dot_general x8, matrix products, proj_step(): jnp.dot(xb, cprob, precision=lax.Precision.HIGHEST)  20 us
    dot_general x1, matrix products, shards(): lax.dot_general(allowed, target_onehot, (((1,), (1,)), ((), ())), precisi...  10.3 us
  transfers between devices with their start and end apart: 2, of which 1 were waited for; matrix products, arithmetic and copies ran while one was open for 1% of the time, Pallas kernels for 0%

commit v1 on v0

v1 whole, which is shorter than its diff:
```python
import functools
import math

import jax
import jax.numpy as jnp
from jax import lax
from jax.experimental import pallas as pl
from jax.experimental.pallas import tpu as pltpu
from jax.sharding import PartitionSpec as P

EPSILON = 0.05
BARRED = -(2.0**100)
LANES = 128
LOG2E = math.log2(math.e)
F32 = jnp.float32
BF16 = jnp.bfloat16
VMEM = pl.BlockSpec(memory_space=pltpu.VMEM)
HBM = pl.BlockSpec(memory_space=pltpu.HBM)


def halves(value):
    high = value.astype(BF16)
    low = (value - high.astype(F32)).astype(BF16)
    return high, low


def onehot(labels, clusters):
    series = lax.broadcasted_iota(jnp.int32, (clusters, labels.shape[1]), 0)
    return series == labels


def barred_by(mask_ref, hot, transposed):
    stop = (1.0 - mask_ref[...].astype(F32)).astype(BF16)
    dims = (((0,), (0,)), ((), ())) if transposed else (((1,), (0,)), ((), ()))
    picked = lax.dot_general(stop, hot.astype(BF16), dims, preferred_element_type=F32)
    return picked * BARRED


def tree(combine, parts):
    parts = list(parts)
    while len(parts) > 1:
        parts = [
            combine(parts[k], parts[k + 1]) if k + 1 < len(parts) else parts[k]
            for k in range(0, len(parts), 2)
        ]
    return parts[0]


def merge(tops):
    peak = tree(jnp.maximum, tops)
    return peak + jnp.log2(tree(jnp.add, [jnp.exp2(part - peak) for part in tops]))


def spread_lanes(dst_ref, rows):
    for k in range(rows.shape[0]):
        square = jnp.broadcast_to(rows[k : k + 1, :], (LANES, LANES))
        dst_ref[k * LANES : (k + 1) * LANES, :] = square.T


def gather_lanes(dst_ref, column_ref):
    for k in range(dst_ref.shape[0]):
        dst_ref[k : k + 1, :] = column_ref[k * LANES : (k + 1) * LANES, :].T[0:1, :]


def online(peak, total, z):
    newer = jnp.maximum(peak, tree(jnp.maximum, z))
    fresh = tree(jnp.add, [jnp.exp2(part - newer) for part in z])
    return newer, total * jnp.exp2(peak - newer) + fresh


def down(peak, total):
    top = jnp.max(peak, 0, keepdims=True)
    return top + jnp.log2(jnp.sum(total * jnp.exp2(peak - top), 0, keepdims=True))


def fetch(pairs, sems):
    copies = [pltpu.make_async_copy(src, dst, sems.at[k]) for k, (src, dst) in enumerate(pairs)]
    for copy in copies:
        copy.start()
    return copies


def first_kernel(
    scale, eps_scale, x_hbm, y_hbm, sl_hbm, tl_hbm, mask_hbm,
    cross_ref, lse_ref, xsq_ref,
    x_ref, y_ref, sl_ref, tl_ref, mask_ref, yop_ref, ysq_ref, sems,
):
    copies = fetch(
        [(y_hbm, y_ref), (tl_hbm, tl_ref), (mask_hbm, mask_ref), (sl_hbm, sl_ref), (x_hbm, x_ref)],
        sems,
    )
    _, rows = x_ref.shape
    cols = y_ref.shape[1]
    clusters = mask_ref.shape[0]
    for copy in copies[:3]:
        copy.wait()
    high, low = halves(y_ref[...] * scale)
    barred = barred_by(mask_ref, onehot(tl_ref[...], clusters), False)
    stacked = jnp.concatenate([high.astype(F32), high.astype(F32), low.astype(F32), barred], 0)
    yop_ref[...] = stacked.T.astype(BF16)
    ysq = jnp.sum(y_ref[...] * y_ref[...], 0, keepdims=True) * (-eps_scale)
    for k in range(cols // LANES):
        square = jnp.broadcast_to(ysq[:, k * LANES : (k + 1) * LANES], (LANES, LANES))
        ysq_ref[k * LANES : (k + 1) * LANES, :] = square.T
    for copy in copies[3:]:
        copy.wait()
    width = min(512, rows)
    narrow = min(256, width)
    depth = min(64, cols)
    base = rows // LANES
    for k in range(cols // LANES):
        lse_ref[base + k : base + k + 1, :] = tl_ref[:, k * LANES : (k + 1) * LANES].astype(F32)

    def chunk(q, unused):
        for half in range(width // narrow):
            line = q * (width // LANES) + half * (narrow // LANES)
            start = pl.multiple_of(q * width + half * narrow, narrow)
            x = x_ref[:, pl.ds(start, narrow)]
            high, low = halves(x)
            hot = onehot(sl_ref[:, pl.ds(start, narrow)], clusters).astype(BF16)
            xop = jnp.concatenate([high, low, high, hot], 0)
            xsq = jnp.sum(x * x, 0, keepdims=True) * eps_scale
            cross = jnp.dot(yop_ref[...], xop, preferred_element_type=F32)
            per = narrow // LANES
            peaks = [jnp.full((8, LANES), 2.0 * BARRED, F32)] * per
            totals = [jnp.zeros((8, LANES), F32)] * per
            for top in range(0, cols, depth):
                for p in range(per):
                    here = pl.ds(pl.multiple_of(start + p * LANES, LANES), LANES)
                    z = []
                    for r in range(top, top + depth, 8):
                        z.append(cross[r : r + 8, p * LANES : (p + 1) * LANES] + ysq_ref[r : r + 8, :])
                        cross_ref[r : r + 8, here] = z[-1]
                    peaks[p], totals[p] = online(peaks[p], totals[p], z)
            for p in range(per):
                xsq_ref[pl.ds(line + p, 1), :] = xsq[:, p * LANES : (p + 1) * LANES]
                lse_ref[pl.ds(line + p, 1), :] = down(peaks[p], totals[p])
        return unused

    lax.fori_loop(0, rows // width, chunk, 0)


def source_shift(parts_refs, xsq_ref, total_rows):
    lines = xsq_ref.shape[0]
    lse = merge([ref[0:lines, :] for ref in parts_refs]) - xsq_ref[...]
    pot = -math.log2(total_rows) - lse
    return pot - xsq_ref[...]


def target_potential(parts_refs, total_cols):
    return -math.log2(total_cols) - merge([ref[...] for ref in parts_refs])


def spread_rows(shift_ref, shift):
    for k in range(shift.shape[0]):
        shift_ref[:, k * LANES : (k + 1) * LANES] = jnp.broadcast_to(shift[k : k + 1, :], (8, LANES))


def col_kernel(total_rows, n_parts, cross_ref, xsq_ref, *refs):
    parts, (lse_ref, pot_ref, shift_ref, peak_ref, mass_ref) = refs[:n_parts], refs[n_parts:]
    cols, rows = cross_ref.shape
    pot_ref[...] = source_shift(parts, xsq_ref, total_rows)
    spread_rows(shift_ref, pot_ref[...])
    deep = min(16, rows // LANES)
    groups = 8

    def block(q, unused):
        for r in range(groups):
            start = pl.ds(pl.multiple_of((q * groups + r) * 8, 8), 8)
            peak = jnp.full((8, LANES), 2.0 * BARRED, F32)
            total = jnp.zeros((8, LANES), F32)
            for c in range(0, rows // LANES, deep):
                lanes = [slice(k * LANES, (k + 1) * LANES) for k in range(c, c + deep)]
                z = [cross_ref[start, at] + shift_ref[:, at] for at in lanes]
                peak, total = online(peak, total, z)
            peak_ref[start, :] = peak
            mass_ref[start, :] = total
        return unused

    lax.fori_loop(0, cols // 8 // groups, block, 0)
    peak = peak_ref[...]
    top = jnp.max(peak, 1, keepdims=True)
    mass = jnp.sum(mass_ref[...] * jnp.exp2(peak - top), 1, keepdims=True)
    mass_ref[...] = jnp.broadcast_to(top + jnp.log2(mass), mass_ref.shape)
    gather_lanes(lse_ref, mass_ref)


def row_kernel(total_cols, n_parts, cross_ref, pot_ref, *refs):
    parts, (plan_ref, sums_ref, g_ref, shift_ref) = refs[:n_parts], refs[n_parts:]
    g_ref[...] = target_potential(parts, total_cols)
    spread_lanes(shift_ref, g_ref[...])
    cols, rows = plan_ref.shape
    width = min(512, rows)

    def block(q, unused):
        for p in range(width // LANES):
            at = pl.ds(pl.multiple_of(q * width + p * LANES, LANES), LANES)
            line = pl.ds(q * (width // LANES) + p, 1)
            pot = jnp.broadcast_to(pot_ref[line, :], (8, LANES))
            totals = []
            for start in range(0, cols, 64):
                t = []
                for r in range(start, start + 64, 8):
                    t.append(jnp.exp2(plan_ref[r : r + 8, at] + (shift_ref[r : r + 8, :] + pot)))
                    plan_ref[r : r + 8, at] = t[-1]
                totals.append(tree(jnp.add, t))
            sums_ref[line, :] = jnp.sum(tree(jnp.add, totals), 0, keepdims=True)
        return unused

    lax.fori_loop(0, rows // width, block, 0)


def weigh(segments, acc_ref, out_ref, mass_ref, rows, tall):
    dims = out_ref.shape[0]

    def block(q, unused):
        span = pl.ds(pl.multiple_of(q * tall, tall), tall)
        first = True
        for make, stack_ref in segments:
            width = stack_ref.shape[0]
            deep = min(2048, width)
            for c in range(0, width, deep):
                highs, lows = [], []
                for k in range(c, c + deep, LANES):
                    high, low = halves(make(span, k))
                    highs.append(high)
                    lows.append(low)
                lhs = jnp.concatenate([jnp.concatenate(highs, 1), jnp.concatenate(lows, 1)], 0)
                part = jnp.dot(lhs, stack_ref[c : c + deep, :], preferred_element_type=F32)
                part = part[:tall] + part[tall:]
                if first:
                    acc_ref[...] = part
                else:
                    acc_ref[...] += part
                first = False
        acc = acc_ref[...]
        mass = acc[:, 2 * dims : 2 * dims + 1]
        weight = acc[:, :dims] + acc[:, dims : 2 * dims]
        if mass_ref is None:
            weight = weight / mass
        else:
            mass_ref[span, :] = jnp.broadcast_to(mass, (tall, LANES))
        out_ref[:, span] = jnp.concatenate([weight, weight], 1).T[:dims, :]
        return unused

    lax.fori_loop(0, rows // tall, block, 0)


def stack_columns(stack_ref, at, high, low):
    dims, n = high.shape
    both = jnp.concatenate([high.astype(F32), low.astype(F32)], 0)
    stack_ref[at, : 2 * dims] = both.T.astype(BF16)
    column = lax.broadcasted_iota(jnp.int32, (n, 16), 1)
    stack_ref[at, 2 * dims :] = jnp.where(column < 8, 1.0, 0.0).astype(BF16)


def stack_kernel(scale, x_hbm, sl_hbm, mask_ref, xst_ref, xop_ref, x_ref, own_ref, sl_ref, sems):
    own, rows = xop_ref.shape[0], x_ref.shape[1]
    start = pl.multiple_of(lax.axis_index("tgt") * own, own)
    mine = pl.ds(start, own)
    copies = fetch(
        [(x_hbm.at[:, mine], own_ref), (sl_hbm.at[:, mine], sl_ref), (x_hbm, x_ref)], sems
    )
    clusters = mask_ref.shape[0]
    for copy in copies[:2]:
        copy.wait()
    high, low = halves(own_ref[...] * scale)
    barred = barred_by(mask_ref, onehot(sl_ref[...], clusters), True)
    stacked = jnp.concatenate([high.astype(F32), low.astype(F32), high.astype(F32), barred], 0)
    xop_ref[...] = stacked.T.astype(BF16)
    copies[2].wait()
    step = min(512, rows)
    for k in range(0, rows, step):
        stack_columns(xst_ref, slice(k, k + step), *halves(x_ref[:, k : k + step]))


def last_col_kernel(total_rows, n_parts, plan_ref, xst_ref, *refs):
    parts = refs[:n_parts]
    sums_ref, weight_ref, scale_ref, mass_ref, acc_ref = refs[n_parts:]
    cols = plan_ref.shape[0]
    tall = acc_ref.shape[0]
    spread_rows(scale_ref, 1.0 / (total_rows * tree(jnp.add, [ref[...] for ref in parts])))

    def make(span, k):
        line = jnp.broadcast_to(scale_ref[0:1, k : k + LANES], (tall, LANES))
        return plan_ref[span, k : k + LANES] * line

    weigh([(make, xst_ref)], acc_ref, weight_ref, mass_ref, cols, tall)
    gather_lanes(sums_ref, mass_ref)


def ready_kernel(eps_scale, n_near, lines, xop_ref, pot_ref, *refs):
    near, far, labels = refs[:n_near], refs[n_near : 2 * n_near], refs[2 * n_near : 3 * n_near]
    cross_ref, yst_ref, yop_ref, ysq_ref, shift_ref = refs[3 * n_near :]
    own, total = cross_ref.shape
    dims, cols = near[0].shape
    clusters = yop_ref.shape[0] - 3 * dims
    tiles = cols // LANES
    place = lax.axis_index("tgt")
    spread_lanes(shift_ref, pot_ref[pl.ds(place * (own // LANES), own // LANES), :])
    for n, ref in enumerate(near + far):
        at = slice(n * cols, (n + 1) * cols)
        y = ref[...]
        high, low = halves(y)
        stack_columns(yst_ref, at, high, low)
        yop_ref[: 3 * dims, at] = jnp.concatenate([high, high, low], 0)
        side, which = divmod(n, n_near)
        for k in range(tiles):
            line = lines + side * tiles + k
            lanes = slice(n * cols + k * LANES, n * cols + (k + 1) * LANES)
            label = labels[which][line : line + 1, :].astype(jnp.int32)
            yop_ref[3 * dims :, lanes] = onehot(label, clusters).astype(BF16)
        ysq = jnp.sum(y * y, 0, keepdims=True) * (-eps_scale)
        ysq_ref[:, at] = jnp.broadcast_to(ysq, (8, cols))
    width = min(512, total)

    def fill(q, unused):
        at = pl.multiple_of(q * width, width)
        cross = jnp.dot(xop_ref[...], yop_ref[:, pl.ds(at, width)], preferred_element_type=F32)
        for p in range(width // LANES):
            here = pl.ds(at + p * LANES, LANES)
            line = jnp.broadcast_to(ysq_ref[0:1, here], (own, LANES))
            cross_ref[:, here] = cross[:, p * LANES : (p + 1) * LANES] + (shift_ref[...] + line)
        return unused

    lax.fori_loop(0, total // width, fill, 0)


def final_kernel(sizes, *refs):
    n = len(sizes)
    crosses, stacks, gs = refs[:n], refs[n : 2 * n], refs[2 * n : -3]
    out_ref, shift_ref, acc_ref = refs[-3:]
    tall = acc_ref.shape[0]
    segments = []
    col = first = 0
    for size, cross_ref, stack_ref in zip(sizes, crosses, stacks):
        base = col
        for side in range(2):
            for g in gs[first : first + size]:
                for k in range(g.shape[1]):
                    shift_ref[:, col : col + LANES] = jnp.broadcast_to(
                        g[side, k : k + 1, :], (8, LANES)
                    )
                    col += LANES
        first += size

        def make(span, k, cross_ref=cross_ref, base=base):
            line = jnp.broadcast_to(shift_ref[0:1, base + k : base + k + LANES], (tall, LANES))
            return jnp.exp2(cross_ref[span, k : k + LANES] + line)

        segments.append((make, stack_ref))
    weigh(segments, acc_ref, out_ref, None, crosses[0].shape[0], tall)


def pairs(size, step):
    return [(k, k ^ step) for k in range(size)]


def swap(value, axis, step):
    return lax.ppermute(value, axis, pairs(lax.axis_size(axis), step))


def params(mib):
    return pltpu.CompilerParams(vmem_limit_bytes=mib << 20)


def in_vmem(value):
    return pltpu.with_memory_space_constraint(value, pltpu.VMEM)


def in_hbm(value):
    return pltpu.with_memory_space_constraint(value, pltpu.HBM)


def shards(source_pca, target_pca, source_labels, target_labels, block_mask):
    dims, rows = source_pca.shape
    cols = target_pca.shape[1]
    nsrc, ntgt = lax.axis_size("src"), lax.axis_size("tgt")
    total_rows, total_cols = rows * nsrc, cols * ntgt
    kappa = LOG2E / EPSILON
    scale, eps_scale = 2.0 * kappa / dims, kappa / dims
    xl, yl = source_labels.reshape(1, rows), target_labels.reshape(1, cols)
    row_lines, col_lines = (rows // LANES, LANES), (cols // LANES, LANES)
    depth = 3 * dims + block_mask.shape[0]
    sds = jax.ShapeDtypeStruct

    steps = list(range(2, ntgt, 2))
    third = max(1, len(steps) // 3)
    legs = [[0], steps[:third], steps[third : 2 * third], steps[2 * third :]]
    near, far = [], []
    for ks in legs:
        near.append([swap(target_pca, "tgt", k) if k else target_pca for k in ks])
        far.append([swap(y, "tgt", 1) for y in near[-1]])

    cross, lse, xsq = pl.pallas_call(
        functools.partial(first_kernel, scale, eps_scale),
        out_shape=(
            pltpu.VMEM((cols, rows), F32),
            sds((row_lines[0] + col_lines[0], LANES), F32),
            sds(row_lines, F32),
        ),
        out_specs=(VMEM,) * 3,
        in_specs=[HBM] * 5,
        scratch_shapes=[
            pltpu.VMEM((dims, rows), F32),
            pltpu.VMEM((dims, cols), F32),
            pltpu.VMEM((1, rows), jnp.int32),
            pltpu.VMEM((1, cols), jnp.int32),
            pltpu.VMEM(block_mask.shape, jnp.int32),
            pltpu.VMEM((cols, depth), BF16),
            pltpu.VMEM((cols, LANES), F32),
            pltpu.SemaphoreType.DMA((5,)),
        ],
        compiler_params=params(12),
        name="first",
    )(*map(in_hbm, (source_pca, target_pca, xl, yl, block_mask)))

    own = rows // ntgt
    xst, xop = pl.pallas_call(
        functools.partial(stack_kernel, scale),
        out_shape=(sds((rows, 2 * dims + 16), BF16), sds((own, depth), BF16)),
        out_specs=(VMEM, VMEM),
        in_specs=[HBM, HBM, VMEM],
        scratch_shapes=[
            pltpu.VMEM((dims, rows), F32),
            pltpu.VMEM((dims, own), F32),
            pltpu.VMEM((1, own), jnp.int32),
            pltpu.SemaphoreType.DMA((3,)),
        ],
        compiler_params=params(8),
        name="stack",
    )(in_hbm(source_pca), in_hbm(xl), block_mask)

    def rows_parts(value, combine):
        other = swap(value, "tgt", 1)
        lines = row_lines[0]
        both = combine([value[:lines], other[:lines]])
        if value.shape[0] > lines:
            both = jnp.concatenate([both, value[lines:], other[lines:]], 0)
        return {0: both} | {k: swap(both, "tgt", k) for k in steps}

    def cols_parts(value):
        return [value] + [swap(value, "src", k) for k in range(1, nsrc)]

    add = functools.partial(tree, jnp.add)
    labelled = rows_parts(lse, merge)
    parts = list(labelled.values())
    col_lse, pots = pl.pallas_call(
        functools.partial(col_kernel, total_rows, len(parts)),
        out_shape=(sds(col_lines, F32), sds(row_lines, F32)),
        out_specs=(VMEM, VMEM),
        in_specs=[VMEM] * (2 + len(parts)),
        scratch_shapes=[
            pltpu.VMEM((8, rows), F32),
            pltpu.VMEM((cols, LANES), F32),
            pltpu.VMEM((cols, LANES), F32),
        ],
        compiler_params=params(8),
        name="col",
    )(in_vmem(cross), xsq, *parts)
    parts = cols_parts(col_lse)
    plan, sums, g = pl.pallas_call(
        functools.partial(row_kernel, total_cols, len(parts)),
        out_shape=(pltpu.VMEM((cols, rows), F32), sds(row_lines, F32), sds(col_lines, F32)),
        out_specs=(VMEM,) * 3,
        in_specs=[VMEM] * (2 + len(parts)),
        scratch_shapes=[pltpu.VMEM((cols, LANES), F32)],
        input_output_aliases={0: 0},
        compiler_params=params(8),
        name="row",
    )(in_vmem(cross), pots, *parts)
    parts = list(rows_parts(sums, add).values())
    mass, weight = pl.pallas_call(
        functools.partial(last_col_kernel, total_rows, len(parts)),
        out_shape=(sds(col_lines, F32), sds((dims, cols), F32)),
        out_specs=(VMEM, VMEM),
        in_specs=[VMEM] * (2 + len(parts)),
        scratch_shapes=[
            pltpu.VMEM((8, rows), F32),
            pltpu.VMEM((cols, LANES), F32),
            pltpu.VMEM((min(256, cols), 2 * dims + 16), F32),
        ],
        compiler_params=params(8),
        name="last_col",
    )(in_vmem(plan), xst, *parts)
    mass = add(cols_parts(mass))
    weights = [weight] + [swap(weight, "src", k) for k in range(1, nsrc)]
    pot = g - math.log2(total_cols) - jnp.log2(mass)

    crosses, stacks, sizes = [], [], [len(ks) for ks in legs]
    for leg, ks in enumerate(legs):
        width = 2 * len(ks) * cols
        own_cross, stack = pl.pallas_call(
            functools.partial(ready_kernel, eps_scale, len(ks), row_lines[0]),
            out_shape=(pltpu.VMEM((own, width), F32), sds((width, 2 * dims + 16), BF16)),
            out_specs=(VMEM, VMEM),
            in_specs=[VMEM] * (2 + 3 * len(ks)),
            scratch_shapes=[
                pltpu.VMEM((depth, width), BF16),
                pltpu.VMEM((8, width), F32),
                pltpu.VMEM((own, LANES), F32),
            ],
            compiler_params=params(4 + (width * (2 * depth + 32) >> 20)),
            name="ready",
        )(xop, pots, *near[leg], *far[leg], *[labelled[k] for k in ks])
        crosses.append(in_vmem(own_cross))
        stacks.append(stack)

    both = jnp.stack([pot, swap(pot, "tgt", 1)])
    gs = [both] + [swap(both, "tgt", k) for k in range(2, ntgt, 2)]
    source_projection = pl.pallas_call(
        functools.partial(final_kernel, sizes),
        out_shape=sds((dims, own), F32),
        out_specs=VMEM,
        in_specs=[VMEM] * (2 * len(sizes) + len(gs)),
        scratch_shapes=[
            pltpu.VMEM((8, total_cols), F32),
            pltpu.VMEM((min(256, own), 2 * dims + 16), F32),
        ],
        compiler_params=params(8),
        name="final",
    )(*crosses, *stacks, *gs)
    target_projection = add(weights) / mass.reshape(1, cols)
    return (source_projection, target_projection)


def solution(mesh):
    placed = (P(None, "src"), P(None, "tgt"), P("src"), P("tgt"), P())
    return jax.shard_map(
        shards,
        mesh=mesh,
        in_specs=placed,
        out_specs=(P(None, ("src", "tgt")), P(None, "tgt")),
        check_vma=False,
    )
```

time: 455 us -> 101 us (0.22)
  matrix products: 203 us -> 0 us
  blocking collectives: 159 us -> 0 us
  Pallas kernels: 0 us -> 38.1 us
  starting transfers between devices: 0.08 us -> 32.8 us
  other arithmetic: 27.1 us -> 0.81 us
  between operations: 14.4 us -> 0.82 us
  waiting for transfers between devices: 39.7 us -> 28.5 us
  local copies, waits for them, and re-layouts: 7.89 us -> 0.01 us
    dot_general x58 -> x0, matrix products: 203 us -> none  [the longest x40 147 us: logits(): lax.dot_general(xb, target_pca, (((0,), (0,)), ((), ())), precision=lax.P...]
    all_gather x8 -> x0, blocking collectives: 89.9 us -> none  [combined_all(): everything = jax.tree.map(lambda part: lax.all_gather(part, axis), value)]
    psum x2 -> x0, waiting for transfers between devices: 39.7 us -> none  [the longest x1 39.6 us: shards(): lax.psum((rmass * factor, rweight * factor[None, :]), 'tgt')]
    pallas_call x0 -> x10, Pallas kernels: none -> 38.1 us  [the longest x4 8.03 us: shards(): pl.pallas_call(functools.partial(ready_kernel, eps_scale, len(ks), row_li...]
    pmax x2 -> x0, blocking collectives: 34.8 us -> none  [the longest x1 25.9 us: shards(): top = lax.pmax(rpeak, 'tgt')]
    psum x2 -> x0, blocking collectives: 34 us -> none  [the longest x1 25.9 us: shards(): lax.psum((rmass * factor, rweight * factor[None, :]), 'tgt')]
    ppermute x0 -> x28, starting transfers between devices: none -> 32.8 us  [swap(): return lax.ppermute(value, axis, pairs(lax.axis_size(axis), step))]
    ppermute x0 -> x28, waiting for transfers between devices: none -> 28.5 us  [swap(): return lax.ppermute(value, axis, pairs(lax.axis_size(axis), step))]
  transfers between devices with their start and end apart: 2 -> 28, of which waited for: 1 -> 11; matrix products, arithmetic and copies ran while one was open for 1% -> 1% of each run, Pallas kernels for 0% -> 10%
where the time goes in v1:
time: 101 us
  Pallas kernels  38.1 us (38%)
  starting transfers between devices  32.8 us (32%)
  waiting for transfers between devices  28.5 us (28%)
    ppermute x28, starting transfers between devices, swap(): return lax.ppermute(value, axis, pairs(lax.axis_size(axis), step))  32.8 us
    ppermute x28, waiting for transfers between devices, swap(): return lax.ppermute(value, axis, pairs(lax.axis_size(axis), step))  28.5 us
    pallas_call x4, Pallas kernels, shards(): pl.pallas_call(functools.partial(ready_kernel, eps_scale, len(ks), row_li...  8.03 us
    pallas_call x1, Pallas kernels, shards(): pl.pallas_call(functools.partial(first_kernel, scale, eps_scale), out_sha...  7.14 us
    pallas_call x1, Pallas kernels, shards(): pl.pallas_call(functools.partial(last_col_kernel, total_rows, len(parts))...  6.34 us
    pallas_call x1, Pallas kernels, shards(): pl.pallas_call(functools.partial(final_kernel, sizes), out_shape=sds((dim...  5.92 us
    pallas_call x1, Pallas kernels, shards(): pl.pallas_call(functools.partial(row_kernel, total_cols, len(parts)), out...  4.91 us
    pallas_call x1, Pallas kernels, shards(): pl.pallas_call(functools.partial(col_kernel, total_rows, len(parts)), out...  3.92 us
  transfers between devices with their start and end apart: 28, of which 11 were waited for; matrix products, arithmetic and copies ran while one was open for 1% of the time, Pallas kernels for 10%

profile of v1, /device:TPU:0, one launch (start us, length us, event | category | flops | bytes accessed | tf_op | source)
XLA Modules:
  0.0 101.0 jit_solution(4951767264941698437)
XLA Ops:
  0.6 7.1 %first.1 = (f32[1024,4096]{1,0:T(8,128)S(1)}, f32[40,128]{1,0:T(8,128)S(1)}, f32[32,128]{1,0:T(8,128)S(1)}) custom-call(f32[64,4096]{1,0:T(8,128)} %x_hbm.3, f32[64,1024]{1,0:T(8,128)} %refs_0_.1, s32[1,4096]{1,0:T(1,128)} %bitcast.5, s32[1,1024]{1,0:T(1,128)} %bitcast.9, s32[64,64]{1,0:T(8,128)} %mask_hbm.1), custom_call_target="tpu_custom_call" | custom-call | tf_op jit(solution)/shard_map/first/pallas_call | solution.py:395
  7.8 0.6 collective-permute-start
  8.3 0.8 collective-permute-done
  9.2 3.0 %collective-permute-start.1 = (f32[48,128]{1,0:T(8,128)S(1)}, f32[48,128]{1,0:T(8,128)S(1)}, u32[]{:S(2)}, u32[]{:S(2)}) collective-permute-start(f32[48,128]{1,0:T(8,128)S(1)} %pad_maximum_fusion.refs_0_.refs_2_), channel_id=1, source_target_pairs={{0,2},{1,3},{2,0},{3,1},{4,6},{5,7},{6,4},{7,5},{8,10},{9,11},{10,... | collective-permute-start | bytes 73736 | tf_op jit(solution)/shard_map/ppermute | solution.py:360
  12.2 2.6 %collective-permute-start.2 = (f32[48,128]{1,0:T(8,128)S(1)}, f32[48,128]{1,0:T(8,128)S(1)}, u32[]{:S(2)}, u32[]{:S(2)}) collective-permute-start(f32[48,128]{1,0:T(8,128)S(1)} %pad_maximum_fusion.refs_0_.refs_2_), channel_id=1, source_target_pairs={{0,4},{1,5},{2,6},{3,7},{4,0},{5,1},{6,2},{7,3},{8,12},{9,13},{10,... | collective-permute-start | bytes 73736 | tf_op jit(solution)/shard_map/ppermute | solution.py:360
  14.8 0.0 collective-permute-start.3
  14.8 0.0 collective-permute-done.1.refs_1_.refs_2_
  14.8 2.3 %collective-permute-done.2.refs_2_ = f32[48,128]{1,0:T(8,128)S(1)} collective-permute-done((f32[48,128]{1,0:T(8,128)S(1)}, f32[48,128]{1,0:T(8,128)S(1)}, u32[]{:S(2)}, u32[]{:S(2)}) %collective-permute-start.2) | collective-permute-done | bytes 24608 | tf_op jit(solution)/shard_map/ppermute | solution.py:360
  17.1 3.3 %collective-permute-done.3.refs_3_.refs_2_ = f32[48,128]{1,0:T(8,128)S(1)} collective-permute-done((f32[48,128]{1,0:T(8,128)S(1)}, f32[48,128]{1,0:T(8,128)S(1)}, u32[]{:S(2)}, u32[]{:S(2)}) %collective-permute-start.3) | collective-permute-done | bytes 24608 | tf_op jit(solution)/shard_map/ppermute | solution.py:360
  20.4 3.9 %col.1 = (f32[8,128]{1,0:T(8,128)S(1)}, f32[32,128]{1,0:T(8,128)S(1)}) custom-call(f32[1024,4096]{1,0:T(8,128)S(1)} %get-tuple-element.23.cross_ref, f32[32,128]{1,0:T(8,128)S(1)} %get-tuple-element.24.xsq_ref, f32[48,128]{1,0:T(8,128)S(1)} %pad_maximum_fusion.refs_0_.refs_2_, f32[48,128]{1,0:T(8,128)S(1)} %collective-permute-done.1.refs_1_.refs_2_, ...), custom_call_target="tpu_custom_call" | custom-call | tf_op jit(solution)/shard_map/col/pallas_call | solution.py:448
  24.3 1.5 %collective-permute-start.11 = (f32[8,128]{1,0:T(8,128)S(1)}, f32[8,128]{1,0:T(8,128)S(1)}, u32[]{:S(2)}, u32[]{:S(2)}) collective-permute-start(f32[8,128]{1,0:T(8,128)S(1)} %get-tuple-element.35.refs_0_), channel_id=1, source_target_pairs={{0,8},{8,0},{16,24},{24,16},{1,9},{9,1},{17,25},{25,17},{2,10},{10... | collective-permute-start | bytes 12296 | tf_op jit(solution)/shard_map/ppermute | solution.py:360
  25.9 1.5 %collective-permute-start.12 = (f32[8,128]{1,0:T(8,128)S(1)}, f32[8,128]{1,0:T(8,128)S(1)}, u32[]{:S(2)}, u32[]{:S(2)}) collective-permute-start(f32[8,128]{1,0:T(8,128)S(1)} %get-tuple-element.35.refs_0_), channel_id=1, source_target_pairs={{0,16},{8,24},{16,0},{24,8},{1,17},{9,25},{17,1},{25,9},{2,18},{10... | collective-permute-start | bytes 12296 | tf_op jit(solution)/shard_map/ppermute | solution.py:360
  27.4 0.5 collective-permute-start.13
  27.9 0.1 collective-permute-done.11.refs_1_
  28.0 1.5 %collective-permute-done.12.refs_2_ = f32[8,128]{1,0:T(8,128)S(1)} collective-permute-done((f32[8,128]{1,0:T(8,128)S(1)}, f32[8,128]{1,0:T(8,128)S(1)}, u32[]{:S(2)}, u32[]{:S(2)}) %collective-permute-start.12) | collective-permute-done | bytes 4128 | tf_op jit(solution)/shard_map/ppermute | solution.py:360
  29.5 2.4 %collective-permute-done.13.refs_3_ = f32[8,128]{1,0:T(8,128)S(1)} collective-permute-done((f32[8,128]{1,0:T(8,128)S(1)}, f32[8,128]{1,0:T(8,128)S(1)}, u32[]{:S(2)}, u32[]{:S(2)}) %collective-permute-start.13) | collective-permute-done | bytes 4128 | tf_op jit(solution)/shard_map/ppermute | solution.py:360
  31.9 4.9 %row.1 = (f32[1024,4096]{1,0:T(8,128)S(1)}, f32[32,128]{1,0:T(8,128)S(1)}, f32[8,128]{1,0:T(8,128)S(1)}) custom-call(f32[1024,4096]{1,0:T(8,128)S(1)} %get-tuple-element.23.cross_ref, f32[32,128]{1,0:T(8,128)S(1)} %get-tuple-element.26.pot_ref, f32[8,128]{1,0:T(8,128)S(1)} %get-tuple-element.35.refs_0_, ...), custom_call_target="tpu_custom_call", output_to_operand_aliasing={{0}: (0, {})} | custom-call | tf_op jit(solution)/shard_map/row/pallas_call | solution.py:462
  36.8 0.1 collective-permute-start.14
  36.9 1.2 %collective-permute-done.14 = f32[32,128]{1,0:T(8,128)S(1)} collective-permute-done((f32[32,128]{1,0:T(8,128)S(1)}, f32[32,128]{1,0:T(8,128)S(1)}, u32[]{:S(2)}, u32[]{:S(2)}) %collective-permute-start.14) | collective-permute-done | bytes 16416 | tf_op jit(solution)/shard_map/ppermute | solution.py:360
  38.1 0.0 collective-permute-start.15
  38.1 0.8 collective-permute-start.16
  38.9 3.6 %collective-permute-start.17 = (f32[32,128]{1,0:T(8,128)S(1)}, f32[32,128]{1,0:T(8,128)S(1)}, u32[]{:S(2)}, u32[]{:S(2)}) collective-permute-start(f32[32,128]{1,0:T(8,128)S(1)} %add.30.refs_0_), channel_id=1, source_target_pairs={{0,6},{1,7},{2,4},{3,5},{4,2},{5,3},{6,0},{7,1},{8,14},{9,15},{10,... | collective-permute-start | bytes 49160 | tf_op jit(solution)/shard_map/ppermute | solution.py:360
  42.5 1.8 %stack.13 = (bf16[4096,144]{1,0:T(8,128)(2,1)S(1)}, bf16[512,256]{1,0:T(8,128)(2,1)S(1)}) custom-call(f32[64,4096]{1,0:T(8,128)} %x_hbm.3, s32[1,4096]{1,0:T(1,128)} %bitcast.6, s32[64,64]{1,0:T(8,128)S(1)} %copy-done.1), custom_call_target="tpu_custom_call" | custom-call | tf_op jit(solution)/shard_map/stack/pallas_call | solution.py:419
  44.3 0.0 collective-permute-done.15.refs_1_
  44.3 0.0 collective-permute-done.16.refs_2_
  44.3 0.1 collective-permute-done.17.refs_3_
  44.4 6.3 %last_col.1 = (f32[8,128]{1,0:T(8,128)S(1)}, f32[64,1024]{1,0:T(8,128)S(1)}) custom-call(f32[1024,4096]{1,0:T(8,128)S(1)} %get-tuple-element.37.plan_ref, bf16[4096,144]{1,0:T(8,128)(2,1)S(1)} %get-tuple-element.38.xst_ref, f32[32,128]{1,0:T(8,128)S(1)} %add.30.refs_0_, f32[32,128]{1,0:T(8,128)S(1)} %collective-permute-done.15.refs_1_, ...), custom_call_target="tpu_custom_call" | custom-call | tf_op jit(solution)/shard_map/last_col/pallas_call | solution.py:473
  50.8 0.6 collective-permute-start.18
  51.4 0.5 collective-permute-start.19
  51.9 2.5 %collective-permute-start.20 = (f32[8,128]{1,0:T(8,128)S(1)}, f32[8,128]{1,0:T(8,128)S(1)}, u32[]{:S(2)}, u32[]{:S(2)}) collective-permute-start(f32[8,128]{1,0:T(8,128)S(1)} %get-tuple-element.40), channel_id=1, source_target_pairs={{0,24},{8,16},{16,8},{24,0},{1,25},{9,17},{17,9},{25,1},{2,26},{10... | collective-permute-start | bytes 12296 | tf_op jit(solution)/shard_map/ppermute | solution.py:360
  54.3 3.6 %collective-permute-start.9 = (f32[64,1024]{1,0:T(8,128)S(1)}, f32[64,1024]{1,0:T(8,128)S(1)}, u32[]{:S(2)}, u32[]{:S(2)}) collective-permute-start(f32[64,1024]{1,0:T(8,128)S(1)} %copy-done), channel_id=1, source_target_pairs={{0,6},{1,7},{2,4},{3,5},{4,2},{5,3},{6,0},{7,1},{8,14},{9,15},{10,... | collective-permute-start | bytes 786440 | tf_op jit(solution)/shard_map/ppermute | solution.py:360
  57.9 0.0 collective-permute-start.7
  57.9 0.0 collective-permute-done.18
  57.9 0.8 collective-permute-start.5
  58.7 0.0 collective-permute-done.19
  58.7 0.0 collective-permute-done.20
  58.7 0.1 collective-permute-start.21
  58.8 0.5 collective-permute-start.4
  59.3 0.7 collective-permute-done.21
  60.0 0.5 collective-permute-start.25
  60.5 4.9 %collective-permute-done.9.refs_0_ = f32[64,1024]{1,0:T(8,128)S(1)} collective-permute-done((f32[64,1024]{1,0:T(8,128)S(1)}, f32[64,1024]{1,0:T(8,128)S(1)}, u32[]{:S(2)}, u32[]{:S(2)}) %collective-permute-start.9) | collective-permute-done | bytes 262176 | tf_op jit(solution)/shard_map/ppermute | solution.py:360
  65.4 0.5 collective-permute-start.26
  65.9 11.1 %collective-permute-done.7.refs_0_ = f32[64,1024]{1,0:T(8,128)S(1)} collective-permute-done((f32[64,1024]{1,0:T(8,128)S(1)}, f32[64,1024]{1,0:T(8,128)S(1)}, u32[]{:S(2)}, u32[]{:S(2)}) %collective-permute-start.7) | collective-permute-done | bytes 262176 | tf_op jit(solution)/shard_map/ppermute | solution.py:360
  77.0 0.5 collective-permute-start.27
  77.5 0.0 collective-permute-done.5.refs_0_
  77.5 0.0 collective-permute-start.10
  77.5 0.0 collective-permute-done.4.refs_1_
  77.5 0.5 collective-permute-start.8
  78.0 0.0 collective-permute-done.25
  78.0 0.1 collective-permute-start.6
  78.1 2.0 %ready.4 = (f32[512,2048]{1,0:T(8,128)S(1)}, bf16[2048,144]{1,0:T(8,128)(2,1)S(1)}) custom-call(bf16[512,256]{1,0:T(8,128)(2,1)S(1)} %get-tuple-element.22.xop_ref, f32[32,128]{1,0:T(8,128)S(1)} %get-tuple-element.26.pot_ref, f32[64,1024]{1,0:T(8,128)S(1)} %copy-done, f32[64,1024]{1,0:T(8,128)S(1)} %collective-permute-done.4.refs_1_, ...), custom_call_target="tpu_custom_call" | custom-call | tf_op jit(solution)/shard_map/ready/pallas_call | solution.py:493
  80.1 0.0 collective-permute-done.26
  80.1 5.7 %collective-permute-start.22 = (f32[2,8,128]{2,1,0:T(8,128)S(1)}, f32[2,8,128]{2,1,0:T(8,128)S(1)}, u32[]{:S(2)}, u32[]{:S(2)}) collective-permute-start(f32[2,8,128]{2,1,0:T(8,128)S(1)} %pad_maximum_fusion.1.refs_8_), channel_id=1, source_target_pairs={{0,2},{1,3},{2,0},{3,1},{4,6},{5,7},{6,4},{7,5},{8,10},{9,11},{10,... | collective-permute-start | bytes 24584 | tf_op jit(solution)/shard_map/ppermute | solution.py:360
  85.9 0.0 collective-permute-done.27
  85.9 0.1 collective-permute-start.23
  86.0 0.0 collective-permute-done.10.refs_1_
  86.0 2.3 %collective-permute-start.24 = (f32[2,8,128]{2,1,0:T(8,128)S(1)}, f32[2,8,128]{2,1,0:T(8,128)S(1)}, u32[]{:S(2)}, u32[]{:S(2)}) collective-permute-start(f32[2,8,128]{2,1,0:T(8,128)S(1)} %pad_maximum_fusion.1.refs_8_), channel_id=1, source_target_pairs={{0,6},{1,7},{2,4},{3,5},{4,2},{5,3},{6,0},{7,1},{8,14},{9,15},{10,... | collective-permute-start | bytes 24584 | tf_op jit(solution)/shard_map/ppermute | solution.py:360
  88.2 0.8 add_divide_fusion
  89.0 2.0 %ready.7 = (f32[512,2048]{1,0:T(8,128)S(1)}, bf16[2048,144]{1,0:T(8,128)(2,1)S(1)}) custom-call(bf16[512,256]{1,0:T(8,128)(2,1)S(1)} %get-tuple-element.22.xop_ref, f32[32,128]{1,0:T(8,128)S(1)} %get-tuple-element.26.pot_ref, f32[64,1024]{1,0:T(8,128)S(1)} %collective-permute-done.9.refs_0_, f32[64,1024]{1,0:T(8,128)S(1)} %collective-permute-done.10.refs_1_, ...), custom_call_target="tpu_custom_call" | custom-call | tf_op jit(solution)/shard_map/ready/pallas_call | solution.py:493
  91.0 0.0 collective-permute-done.8.refs_1_
  91.0 2.0 %ready.6 = (f32[512,2048]{1,0:T(8,128)S(1)}, bf16[2048,144]{1,0:T(8,128)(2,1)S(1)}) custom-call(bf16[512,256]{1,0:T(8,128)(2,1)S(1)} %get-tuple-element.22.xop_ref, f32[32,128]{1,0:T(8,128)S(1)} %get-tuple-element.26.pot_ref, f32[64,1024]{1,0:T(8,128)S(1)} %collective-permute-done.7.refs_0_, f32[64,1024]{1,0:T(8,128)S(1)} %collective-permute-done.8.refs_1_, ...), custom_call_target="tpu_custom_call" | custom-call | tf_op jit(solution)/shard_map/ready/pallas_call | solution.py:493
  93.1 2.0 %ready.5 = (f32[512,2048]{1,0:T(8,128)S(1)}, bf16[2048,144]{1,0:T(8,128)(2,1)S(1)}) custom-call(bf16[512,256]{1,0:T(8,128)(2,1)S(1)} %get-tuple-element.22.xop_ref, f32[32,128]{1,0:T(8,128)S(1)} %get-tuple-element.26.pot_ref, f32[64,1024]{1,0:T(8,128)S(1)} %collective-permute-done.5.refs_0_, f32[64,1024]{1,0:T(8,128)S(1)} %collective-permute-done.6.refs_1_, ...), custom_call_target="tpu_custom_call" | custom-call | tf_op jit(solution)/shard_map/ready/pallas_call | solution.py:493
  95.1 0.0 collective-permute-done.22.refs_9_
  95.1 5.9 %final.1 = f32[64,512]{1,0:T(8,128)} custom-call(f32[512,2048]{1,0:T(8,128)S(1)} %get-tuple-element.27.refs_0_, f32[512,2048]{1,0:T(8,128)S(1)} %get-tuple-element.28.refs_1_, f32[512,2048]{1,0:T(8,128)S(1)} %get-tuple-element.29.refs_2_, f32[512,2048]{1,0:T(8,128)S(1)} %get-tuple-element.30.refs_3_, bf16[2048,144]{1,0:T(8,128)(2,1)S(1)} %get-tuple-element.31.refs_4_, ...), custom_call_target="tpu_custom_call" | custom-call | tf_op jit(solution)/shard_map/final/pallas_call | solution.py:511
  (14 shorter events, 0.1 us)
Async XLA Ops:
  7.8 1.4 %collective-permute-start = (f32[40,128]{1,0:T(8,128)S(1)}, f32[40,128]{1,0:T(8,128)S(1)}, u32[]{:S(2)}, u32[]{:S(2)}) collective-permute-start(f32[40,128]{1,0:T(8,128)S(1)} %get-tuple-element.25), channel_id=1, source_target_pairs={{0,1},{1,0},{2,3},{3,2},{4,5},{5,4},{6,7},{7,6},{8,9},{9,8},{10,11... | collective-permute-start | bytes 61448 | tf_op jit(solution)/shard_map/ppermute | solution.py:360
  9.2 5.6 %collective-permute-start.1 = (f32[48,128]{1,0:T(8,128)S(1)}, f32[48,128]{1,0:T(8,128)S(1)}, u32[]{:S(2)}, u32[]{:S(2)}) collective-permute-start(f32[48,128]{1,0:T(8,128)S(1)} %pad_maximum_fusion.refs_0_.refs_2_), channel_id=1, source_target_pairs={{0,2},{1,3},{2,0},{3,1},{4,6},{5,7},{6,4},{7,5},{8,10},{9,11},{10,... | collective-permute-start | bytes 73736 | tf_op jit(solution)/shard_map/ppermute | solution.py:360
  12.2 4.9 %collective-permute-start.2 = (f32[48,128]{1,0:T(8,128)S(1)}, f32[48,128]{1,0:T(8,128)S(1)}, u32[]{:S(2)}, u32[]{:S(2)}) collective-permute-start(f32[48,128]{1,0:T(8,128)S(1)} %pad_maximum_fusion.refs_0_.refs_2_), channel_id=1, source_target_pairs={{0,4},{1,5},{2,6},{3,7},{4,0},{5,1},{6,2},{7,3},{8,12},{9,13},{10,... | collective-permute-start | bytes 73736 | tf_op jit(solution)/shard_map/ppermute | solution.py:360
  14.8 5.6 %collective-permute-start.3 = (f32[48,128]{1,0:T(8,128)S(1)}, f32[48,128]{1,0:T(8,128)S(1)}, u32[]{:S(2)}, u32[]{:S(2)}) collective-permute-start(f32[48,128]{1,0:T(8,128)S(1)} %pad_maximum_fusion.refs_0_.refs_2_), channel_id=1, source_target_pairs={{0,6},{1,7},{2,4},{3,5},{4,2},{5,3},{6,0},{7,1},{8,14},{9,15},{10,... | collective-permute-start | bytes 73736 | tf_op jit(solution)/shard_map/ppermute | solution.py:360
  24.3 3.7 %collective-permute-start.11 = (f32[8,128]{1,0:T(8,128)S(1)}, f32[8,128]{1,0:T(8,128)S(1)}, u32[]{:S(2)}, u32[]{:S(2)}) collective-permute-start(f32[8,128]{1,0:T(8,128)S(1)} %get-tuple-element.35.refs_0_), channel_id=1, source_target_pairs={{0,8},{8,0},{16,24},{24,16},{1,9},{9,1},{17,25},{25,17},{2,10},{10... | collective-permute-start | bytes 12296 | tf_op jit(solution)/shard_map/ppermute | solution.py:360
  25.9 3.6 %collective-permute-start.12 = (f32[8,128]{1,0:T(8,128)S(1)}, f32[8,128]{1,0:T(8,128)S(1)}, u32[]{:S(2)}, u32[]{:S(2)}) collective-permute-start(f32[8,128]{1,0:T(8,128)S(1)} %get-tuple-element.35.refs_0_), channel_id=1, source_target_pairs={{0,16},{8,24},{16,0},{24,8},{1,17},{9,25},{17,1},{25,9},{2,18},{10... | collective-permute-start | bytes 12296 | tf_op jit(solution)/shard_map/ppermute | solution.py:360
  27.4 4.5 %collective-permute-start.13 = (f32[8,128]{1,0:T(8,128)S(1)}, f32[8,128]{1,0:T(8,128)S(1)}, u32[]{:S(2)}, u32[]{:S(2)}) collective-permute-start(f32[8,128]{1,0:T(8,128)S(1)} %get-tuple-element.35.refs_0_), channel_id=1, source_target_pairs={{0,24},{8,16},{16,8},{24,0},{1,25},{9,17},{17,9},{25,1},{2,26},{10... | collective-permute-start | bytes 12296 | tf_op jit(solution)/shard_map/ppermute | solution.py:360
  31.9 10.6 %copy-start.1 = (s32[64,64]{1,0:T(8,128)S(1)}, s32[64,64]{1,0:T(8,128)}, u32[]{:S(2)}) copy-start(s32[64,64]{1,0:T(8,128)} %mask_hbm.1) | copy-start | bytes 49156
  36.8 1.2 %collective-permute-start.14 = (f32[32,128]{1,0:T(8,128)S(1)}, f32[32,128]{1,0:T(8,128)S(1)}, u32[]{:S(2)}, u32[]{:S(2)}) collective-permute-start(f32[32,128]{1,0:T(8,128)S(1)} %get-tuple-element.39), channel_id=1, source_target_pairs={{0,1},{1,0},{2,3},{3,2},{4,5},{5,4},{6,7},{7,6},{8,9},{9,8},{10,11... | collective-permute-start | bytes 49160 | tf_op jit(solution)/shard_map/ppermute | solution.py:360
  38.1 6.2 %collective-permute-start.15 = (f32[32,128]{1,0:T(8,128)S(1)}, f32[32,128]{1,0:T(8,128)S(1)}, u32[]{:S(2)}, u32[]{:S(2)}) collective-permute-start(f32[32,128]{1,0:T(8,128)S(1)} %add.30.refs_0_), channel_id=1, source_target_pairs={{0,2},{1,3},{2,0},{3,1},{4,6},{5,7},{6,4},{7,5},{8,10},{9,11},{10,... | collective-permute-start | bytes 49160 | tf_op jit(solution)/shard_map/ppermute | solution.py:360
  38.1 6.2 %collective-permute-start.16 = (f32[32,128]{1,0:T(8,128)S(1)}, f32[32,128]{1,0:T(8,128)S(1)}, u32[]{:S(2)}, u32[]{:S(2)}) collective-permute-start(f32[32,128]{1,0:T(8,128)S(1)} %add.30.refs_0_), channel_id=1, source_target_pairs={{0,4},{1,5},{2,6},{3,7},{4,0},{5,1},{6,2},{7,3},{8,12},{9,13},{10,... | collective-permute-start | bytes 49160 | tf_op jit(solution)/shard_map/ppermute | solution.py:360
  38.9 5.5 %collective-permute-start.17 = (f32[32,128]{1,0:T(8,128)S(1)}, f32[32,128]{1,0:T(8,128)S(1)}, u32[]{:S(2)}, u32[]{:S(2)}) collective-permute-start(f32[32,128]{1,0:T(8,128)S(1)} %add.30.refs_0_), channel_id=1, source_target_pairs={{0,6},{1,7},{2,4},{3,5},{4,2},{5,3},{6,0},{7,1},{8,14},{9,15},{10,... | collective-permute-start | bytes 49160 | tf_op jit(solution)/shard_map/ppermute | solution.py:360
  44.4 9.9 %copy-start = (f32[64,1024]{1,0:T(8,128)S(1)}, f32[64,1024]{1,0:T(8,128)}, u32[]{:S(2)}) copy-start(f32[64,1024]{1,0:T(8,128)} %refs_0_.1) | copy-start | bytes 786436
  50.8 7.1 %collective-permute-start.18 = (f32[8,128]{1,0:T(8,128)S(1)}, f32[8,128]{1,0:T(8,128)S(1)}, u32[]{:S(2)}, u32[]{:S(2)}) collective-permute-start(f32[8,128]{1,0:T(8,128)S(1)} %get-tuple-element.40), channel_id=1, source_target_pairs={{0,8},{8,0},{16,24},{24,16},{1,9},{9,1},{17,25},{25,17},{2,10},{10... | collective-permute-start | bytes 12296 | tf_op jit(solution)/shard_map/ppermute | solution.py:360
  51.4 7.4 %collective-permute-start.19 = (f32[8,128]{1,0:T(8,128)S(1)}, f32[8,128]{1,0:T(8,128)S(1)}, u32[]{:S(2)}, u32[]{:S(2)}) collective-permute-start(f32[8,128]{1,0:T(8,128)S(1)} %get-tuple-element.40), channel_id=1, source_target_pairs={{0,16},{8,24},{16,0},{24,8},{1,17},{9,25},{17,1},{25,9},{2,18},{10... | collective-permute-start | bytes 12296 | tf_op jit(solution)/shard_map/ppermute | solution.py:360
  51.9 6.9 %collective-permute-start.20 = (f32[8,128]{1,0:T(8,128)S(1)}, f32[8,128]{1,0:T(8,128)S(1)}, u32[]{:S(2)}, u32[]{:S(2)}) collective-permute-start(f32[8,128]{1,0:T(8,128)S(1)} %get-tuple-element.40), channel_id=1, source_target_pairs={{0,24},{8,16},{16,8},{24,0},{1,25},{9,17},{17,9},{25,1},{2,26},{10... | collective-permute-start | bytes 12296 | tf_op jit(solution)/shard_map/ppermute | solution.py:360
  54.3 11.1 %collective-permute-start.9 = (f32[64,1024]{1,0:T(8,128)S(1)}, f32[64,1024]{1,0:T(8,128)S(1)}, u32[]{:S(2)}, u32[]{:S(2)}) collective-permute-start(f32[64,1024]{1,0:T(8,128)S(1)} %copy-done), channel_id=1, source_target_pairs={{0,6},{1,7},{2,4},{3,5},{4,2},{5,3},{6,0},{7,1},{8,14},{9,15},{10,... | collective-permute-start | bytes 786440 | tf_op jit(solution)/shard_map/ppermute | solution.py:360
  57.9 19.1 %collective-permute-start.7 = (f32[64,1024]{1,0:T(8,128)S(1)}, f32[64,1024]{1,0:T(8,128)S(1)}, u32[]{:S(2)}, u32[]{:S(2)}) collective-permute-start(f32[64,1024]{1,0:T(8,128)S(1)} %copy-done), channel_id=1, source_target_pairs={{0,4},{1,5},{2,6},{3,7},{4,0},{5,1},{6,2},{7,3},{8,12},{9,13},{10,... | collective-permute-start | bytes 786440 | tf_op jit(solution)/shard_map/ppermute | solution.py:360
  57.9 19.6 %collective-permute-start.5 = (f32[64,1024]{1,0:T(8,128)S(1)}, f32[64,1024]{1,0:T(8,128)S(1)}, u32[]{:S(2)}, u32[]{:S(2)}) collective-permute-start(f32[64,1024]{1,0:T(8,128)S(1)} %copy-done), channel_id=1, source_target_pairs={{0,2},{1,3},{2,0},{3,1},{4,6},{5,7},{6,4},{7,5},{8,10},{9,11},{10,... | collective-permute-start | bytes 786440 | tf_op jit(solution)/shard_map/ppermute | solution.py:360
  58.7 1.2 %collective-permute-start.21 = (f32[8,128]{1,0:T(8,128)S(1)}, f32[8,128]{1,0:T(8,128)S(1)}, u32[]{:S(2)}, u32[]{:S(2)}) collective-permute-start(f32[8,128]{1,0:T(8,128)S(1)} %get-tuple-element.42), channel_id=1, source_target_pairs={{0,1},{1,0},{2,3},{3,2},{4,5},{5,4},{6,7},{7,6},{8,9},{9,8},{10,11... | collective-permute-start | bytes 12296 | tf_op jit(solution)/shard_map/ppermute | solution.py:360
  58.8 18.7 %collective-permute-start.4 = (f32[64,1024]{1,0:T(8,128)S(1)}, f32[64,1024]{1,0:T(8,128)S(1)}, u32[]{:S(2)}, u32[]{:S(2)}) collective-permute-start(f32[64,1024]{1,0:T(8,128)S(1)} %copy-done), channel_id=1, source_target_pairs={{0,1},{1,0},{2,3},{3,2},{4,5},{5,4},{6,7},{7,6},{8,9},{9,8},{10,11... | collective-permute-start | bytes 786440 | tf_op jit(solution)/shard_map/ppermute | solution.py:360
  60.0 18.1 %collective-permute-start.25 = (f32[64,1024]{1,0:T(8,128)S(1)}, f32[64,1024]{1,0:T(8,128)S(1)}, u32[]{:S(2)}, u32[]{:S(2)}) collective-permute-start(f32[64,1024]{1,0:T(8,128)S(1)} %get-tuple-element.41), channel_id=1, source_target_pairs={{0,8},{8,0},{16,24},{24,16},{1,9},{9,1},{17,25},{25,17},{2,10},{10... | collective-permute-start | bytes 786440 | tf_op jit(solution)/shard_map/ppermute | solution.py:360
  65.4 14.7 %collective-permute-start.26 = (f32[64,1024]{1,0:T(8,128)S(1)}, f32[64,1024]{1,0:T(8,128)S(1)}, u32[]{:S(2)}, u32[]{:S(2)}) collective-permute-start(f32[64,1024]{1,0:T(8,128)S(1)} %get-tuple-element.41), channel_id=1, source_target_pairs={{0,16},{8,24},{16,0},{24,8},{1,17},{9,25},{17,1},{25,9},{2,18},{10... | collective-permute-start | bytes 786440 | tf_op jit(solution)/shard_map/ppermute | solution.py:360
  77.0 8.8 %collective-permute-start.27 = (f32[64,1024]{1,0:T(8,128)S(1)}, f32[64,1024]{1,0:T(8,128)S(1)}, u32[]{:S(2)}, u32[]{:S(2)}) collective-permute-start(f32[64,1024]{1,0:T(8,128)S(1)} %get-tuple-element.41), channel_id=1, source_target_pairs={{0,24},{8,16},{16,8},{24,0},{1,25},{9,17},{17,9},{25,1},{2,26},{10... | collective-permute-start | bytes 786440 | tf_op jit(solution)/shard_map/ppermute | solution.py:360
  77.5 8.5 %collective-permute-start.10 = (f32[64,1024]{1,0:T(8,128)S(1)}, f32[64,1024]{1,0:T(8,128)S(1)}, u32[]{:S(2)}, u32[]{:S(2)}) collective-permute-start(f32[64,1024]{1,0:T(8,128)S(1)} %collective-permute-done.9.refs_0_), channel_id=1, source_target_pairs={{0,1},{1,0},{2,3},{3,2},{4,5},{5,4},{6,7},{7,6},{8,9},{9,8},{10,11... | collective-permute-start | bytes 786440 | tf_op jit(solution)/shard_map/ppermute | solution.py:360
  77.5 13.5 %collective-permute-start.8 = (f32[64,1024]{1,0:T(8,128)S(1)}, f32[64,1024]{1,0:T(8,128)S(1)}, u32[]{:S(2)}, u32[]{:S(2)}) collective-permute-start(f32[64,1024]{1,0:T(8,128)S(1)} %collective-permute-done.7.refs_0_), channel_id=1, source_target_pairs={{0,1},{1,0},{2,3},{3,2},{4,5},{5,4},{6,7},{7,6},{8,9},{9,8},{10,11... | collective-permute-start | bytes 786440 | tf_op jit(solution)/shard_map/ppermute | solution.py:360
  78.0 15.0 %collective-permute-start.6 = (f32[64,1024]{1,0:T(8,128)S(1)}, f32[64,1024]{1,0:T(8,128)S(1)}, u32[]{:S(2)}, u32[]{:S(2)}) collective-permute-start(f32[64,1024]{1,0:T(8,128)S(1)} %collective-permute-done.5.refs_0_), channel_id=1, source_target_pairs={{0,1},{1,0},{2,3},{3,2},{4,5},{5,4},{6,7},{7,6},{8,9},{9,8},{10,11... | collective-permute-start | bytes 786440 | tf_op jit(solution)/shard_map/ppermute | solution.py:360
  80.1 15.0 %collective-permute-start.22 = (f32[2,8,128]{2,1,0:T(8,128)S(1)}, f32[2,8,128]{2,1,0:T(8,128)S(1)}, u32[]{:S(2)}, u32[]{:S(2)}) collective-permute-start(f32[2,8,128]{2,1,0:T(8,128)S(1)} %pad_maximum_fusion.1.refs_8_), channel_id=1, source_target_pairs={{0,2},{1,3},{2,0},{3,1},{4,6},{5,7},{6,4},{7,5},{8,10},{9,11},{10,... | collective-permute-start | bytes 24584 | tf_op jit(solution)/shard_map/ppermute | solution.py:360
  85.9 9.2 %collective-permute-start.23 = (f32[2,8,128]{2,1,0:T(8,128)S(1)}, f32[2,8,128]{2,1,0:T(8,128)S(1)}, u32[]{:S(2)}, u32[]{:S(2)}) collective-permute-start(f32[2,8,128]{2,1,0:T(8,128)S(1)} %pad_maximum_fusion.1.refs_8_), channel_id=1, source_target_pairs={{0,4},{1,5},{2,6},{3,7},{4,0},{5,1},{6,2},{7,3},{8,12},{9,13},{10,... | collective-permute-start | bytes 24584 | tf_op jit(solution)/shard_map/ppermute | solution.py:360
  86.0 9.1 %collective-permute-start.24 = (f32[2,8,128]{2,1,0:T(8,128)S(1)}, f32[2,8,128]{2,1,0:T(8,128)S(1)}, u32[]{:S(2)}, u32[]{:S(2)}) collective-permute-start(f32[2,8,128]{2,1,0:T(8,128)S(1)} %pad_maximum_fusion.1.refs_8_), channel_id=1, source_target_pairs={{0,6},{1,7},{2,4},{3,5},{4,2},{5,3},{6,0},{7,1},{8,14},{9,15},{10,... | collective-permute-start | bytes 24584 | tf_op jit(solution)/shard_map/ppermute | solution.py:360

commit v2 on v1

--- a/solution.py
+++ b/solution.py
@@ -104,37 +104,39 @@
         ysq_ref[k * LANES : (k + 1) * LANES, :] = square.T
     for copy in copies[3:]:
         copy.wait()
-    width = min(512, rows)
+    width = min(1024, rows)
     narrow = min(256, width)
-    depth = min(64, cols)
+    depth = min(32, cols)
     base = rows // LANES
     for k in range(cols // LANES):
         lse_ref[base + k : base + k + 1, :] = tl_ref[:, k * LANES : (k + 1) * LANES].astype(F32)
 
     def chunk(q, unused):
-        for half in range(width // narrow):
-            line = q * (width // LANES) + half * (narrow // LANES)
-            start = pl.multiple_of(q * width + half * narrow, narrow)
-            x = x_ref[:, pl.ds(start, narrow)]
+        base = pl.multiple_of(q * width, width)
+        here = cross_ref.at[:, pl.ds(base, width)]
+        xs = x_ref.at[:, pl.ds(base, width)]
+        labels = sl_ref.at[:, pl.ds(base, width)]
+        per = narrow // LANES
+        for n in range(0, width, narrow):
+            x = xs[:, n : n + narrow]
             high, low = halves(x)
-            hot = onehot(sl_ref[:, pl.ds(start, narrow)], clusters).astype(BF16)
+            hot = onehot(labels[:, n : n + narrow], clusters).astype(BF16)
             xop = jnp.concatenate([high, low, high, hot], 0)
             xsq = jnp.sum(x * x, 0, keepdims=True) * eps_scale
             cross = jnp.dot(yop_ref[...], xop, preferred_element_type=F32)
-            per = narrow // LANES
             peaks = [jnp.full((8, LANES), 2.0 * BARRED, F32)] * per
             totals = [jnp.zeros((8, LANES), F32)] * per
             for top in range(0, cols, depth):
                 for p in range(per):
-                    here = pl.ds(pl.multiple_of(start + p * LANES, LANES), LANES)
                     z = []
                     for r in range(top, top + depth, 8):
                         z.append(cross[r : r + 8, p * LANES : (p + 1) * LANES] + ysq_ref[r : r + 8, :])
-                        cross_ref[r : r + 8, here] = z[-1]
+                        here[r : r + 8, n + p * LANES : n + (p + 1) * LANES] = z[-1]
                     peaks[p], totals[p] = online(peaks[p], totals[p], z)
             for p in range(per):
-                xsq_ref[pl.ds(line + p, 1), :] = xsq[:, p * LANES : (p + 1) * LANES]
-                lse_ref[pl.ds(line + p, 1), :] = down(peaks[p], totals[p])
+                line = pl.ds(q * (width // LANES) + n // LANES + p, 1)
+                xsq_ref[line, :] = xsq[:, p * LANES : (p + 1) * LANES]
+                lse_ref[line, :] = down(peaks[p], totals[p])
         return unused
 
     lax.fori_loop(0, rows // width, chunk, 0)
@@ -193,100 +195,119 @@
     width = min(512, rows)
 
     def block(q, unused):
-        for p in range(width // LANES):
-            at = pl.ds(pl.multiple_of(q * width + p * LANES, LANES), LANES)
-            line = pl.ds(q * (width // LANES) + p, 1)
-            pot = jnp.broadcast_to(pot_ref[line, :], (8, LANES))
-            totals = []
-            for start in range(0, cols, 64):
-                t = []
-                for r in range(start, start + 64, 8):
-                    t.append(jnp.exp2(plan_ref[r : r + 8, at] + (shift_ref[r : r + 8, :] + pot)))
-                    plan_ref[r : r + 8, at] = t[-1]
-                totals.append(tree(jnp.add, t))
-            sums_ref[line, :] = jnp.sum(tree(jnp.add, totals), 0, keepdims=True)
+        tiles = range(width // LANES)
+        here = plan_ref.at[:, pl.ds(pl.multiple_of(q * width, width), width)]
+        lines = q * (width // LANES)
+        pot = [jnp.broadcast_to(pot_ref[pl.ds(lines + p, 1), :], (8, LANES)) for p in tiles]
+        totals = [[] for p in tiles]
+        for start in range(0, cols, 32):
+            t = [[] for p in tiles]
+            for r in range(start, start + 32, 8):
+                for p in tiles:
+                    at = slice(p * LANES, (p + 1) * LANES)
+                    part = jnp.exp2(here[r : r + 8, at] + (shift_ref[r : r + 8, :] + pot[p]))
+                    here[r : r + 8, at] = part
+                    t[p].append(part)
+            for p in tiles:
+                totals[p] = [tree(jnp.add, totals[p] + t[p])]
+        for p in tiles:
+            sums_ref[pl.ds(lines + p, 1), :] = jnp.sum(totals[p][0], 0, keepdims=True)
         return unused
 
     lax.fori_loop(0, rows // width, block, 0)
 
 
-def weigh(segments, acc_ref, out_ref, mass_ref, rows, tall):
+def weigh(segments, high_ref, low_ref, out_ref, mass_ref, rows):
     dims = out_ref.shape[0]
+    tall = high_ref.shape[1]
+    short = low_ref.shape[0]
+    lanes = (((1,), (1,)), ((), ()))
 
     def block(q, unused):
         span = pl.ds(pl.multiple_of(q * tall, tall), tall)
         first = True
         for make, stack_ref in segments:
-            width = stack_ref.shape[0]
-            deep = min(2048, width)
+            width = stack_ref.shape[1]
+            deep = min(1024, width)
             for c in range(0, width, deep):
                 highs, lows = [], []
                 for k in range(c, c + deep, LANES):
                     high, low = halves(make(span, k))
                     highs.append(high)
                     lows.append(low)
-                lhs = jnp.concatenate([jnp.concatenate(highs, 1), jnp.concatenate(lows, 1)], 0)
-                part = jnp.dot(lhs, stack_ref[c : c + deep, :], preferred_element_type=F32)
-                part = part[:tall] + part[tall:]
+                stack = stack_ref[:, c : c + deep]
+                with_high = lax.dot_general(
+                    stack, jnp.concatenate(highs, 1), lanes, preferred_element_type=F32
+                )
+                with_low = lax.dot_general(
+                    stack[:short], jnp.concatenate(lows, 1), lanes, preferred_element_type=F32
+                )
                 if first:
-                    acc_ref[...] = part
+                    high_ref[...] = with_high
+                    low_ref[...] = with_low
                 else:
-                    acc_ref[...] += part
+                    high_ref[...] += with_high
+                    low_ref[...] += with_low
                 first = False
-        acc = acc_ref[...]
-        mass = acc[:, 2 * dims : 2 * dims + 1]
-        weight = acc[:, :dims] + acc[:, dims : 2 * dims]
+        mass = high_ref[dims : dims + 1, :] + low_ref[dims : dims + 1, :]
+        weight = (high_ref[:dims, :] + low_ref[:dims, :]) + high_ref[short:, :]
         if mass_ref is None:
             weight = weight / mass
         else:
-            mass_ref[span, :] = jnp.broadcast_to(mass, (tall, LANES))
-        out_ref[:, span] = jnp.concatenate([weight, weight], 1).T[:dims, :]
+            for k in range(tall // LANES):
+                line = pl.ds(q * (tall // LANES) + k, 1)
+                mass_ref[line, :] = mass[:, k * LANES : (k + 1) * LANES]
+        out_ref[:, span] = weight
         return unused
 
     lax.fori_loop(0, rows // tall, block, 0)
 
 
-def stack_columns(stack_ref, at, high, low):
-    dims, n = high.shape
-    both = jnp.concatenate([high.astype(F32), low.astype(F32)], 0)
-    stack_ref[at, : 2 * dims] = both.T.astype(BF16)
-    column = lax.broadcasted_iota(jnp.int32, (n, 16), 1)
-    stack_ref[at, 2 * dims :] = jnp.where(column < 8, 1.0, 0.0).astype(BF16)
-
-
-def stack_kernel(scale, x_hbm, sl_hbm, mask_ref, xst_ref, xop_ref, x_ref, own_ref, sl_ref, sems):
+def stack_lines(stack_ref, at, high, low):
+    _, n = high.shape
+    stack_ref[:, at] = jnp.concatenate([high, jnp.ones((16, n), BF16), low], 0)
+
+
+def stack_kernel(
+    scale, x_hbm, sl_hbm, mask_hbm, xst_ref, xop_ref, x_ref, own_ref, sl_ref, mask_ref, sems
+):
     own, rows = xop_ref.shape[0], x_ref.shape[1]
     start = pl.multiple_of(lax.axis_index("tgt") * own, own)
     mine = pl.ds(start, own)
     copies = fetch(
-        [(x_hbm.at[:, mine], own_ref), (sl_hbm.at[:, mine], sl_ref), (x_hbm, x_ref)], sems
+        [
+            (x_hbm.at[:, mine], own_ref),
+            (sl_hbm.at[:, mine], sl_ref),
+            (mask_hbm, mask_ref),
+            (x_hbm, x_ref),
+        ],
+        sems,
     )
     clusters = mask_ref.shape[0]
-    for copy in copies[:2]:
+    for copy in copies[:3]:
         copy.wait()
     high, low = halves(own_ref[...] * scale)
     barred = barred_by(mask_ref, onehot(sl_ref[...], clusters), True)
     stacked = jnp.concatenate([high.astype(F32), low.astype(F32), high.astype(F32), barred], 0)
     xop_ref[...] = stacked.T.astype(BF16)
-    copies[2].wait()
+    copies[3].wait()
     step = min(512, rows)
     for k in range(0, rows, step):
-        stack_columns(xst_ref, slice(k, k + step), *halves(x_ref[:, k : k + step]))
+        stack_lines(xst_ref, slice(k, k + step), *halves(x_ref[:, k : k + step]))
 
 
 def last_col_kernel(total_rows, n_parts, plan_ref, xst_ref, *refs):
     parts = refs[:n_parts]
-    sums_ref, weight_ref, scale_ref, mass_ref, acc_ref = refs[n_parts:]
+    sums_ref, weight_ref, scale_ref, high_ref, low_ref = refs[n_parts:]
     cols = plan_ref.shape[0]
-    tall = acc_ref.shape[0]
+    tall = high_ref.shape[1]
     spread_rows(scale_ref, 1.0 / (total_rows * tree(jnp.add, [ref[...] for ref in parts])))
 
     def make(span, k):
         line = jnp.broadcast_to(scale_ref[0:1, k : k + LANES], (tall, LANES))
         return plan_ref[span, k : k + LANES] * line
 
-    weigh([(make, xst_ref)], acc_ref, weight_ref, mass_ref, cols, tall)
-    gather_lanes(sums_ref, mass_ref)
+    weigh([(make, xst_ref)], high_ref, low_ref, weight_ref, sums_ref, cols)
 
 
 def ready_kernel(eps_scale, n_near, lines, xop_ref, pot_ref, *refs):
@@ -302,7 +323,7 @@
         at = slice(n * cols, (n + 1) * cols)
         y = ref[...]
         high, low = halves(y)
-        stack_columns(yst_ref, at, high, low)
+        stack_lines(yst_ref, at, high, low)
         yop_ref[: 3 * dims, at] = jnp.concatenate([high, high, low], 0)
         side, which = divmod(n, n_near)
         for k in range(tiles):
@@ -312,7 +333,7 @@
             yop_ref[3 * dims :, lanes] = onehot(label, clusters).astype(BF16)
         ysq = jnp.sum(y * y, 0, keepdims=True) * (-eps_scale)
         ysq_ref[:, at] = jnp.broadcast_to(ysq, (8, cols))
-    width = min(512, total)
+    width = min(1024, total)
 
     def fill(q, unused):
         at = pl.multiple_of(q * width, width)
@@ -328,9 +349,9 @@
 
 def final_kernel(sizes, *refs):
     n = len(sizes)
-    crosses, stacks, gs = refs[:n], refs[n : 2 * n], refs[2 * n : -3]
-    out_ref, shift_ref, acc_ref = refs[-3:]
-    tall = acc_ref.shape[0]
+    crosses, stacks, gs = refs[:n], refs[n : 2 * n], refs[2 * n : -4]
+    out_ref, shift_ref, high_ref, low_ref = refs[-4:]
+    tall = high_ref.shape[1]
     segments = []
     col = first = 0
     for size, cross_ref, stack_ref in zip(sizes, crosses, stacks):
@@ -349,7 +370,7 @@
             return jnp.exp2(cross_ref[span, k : k + LANES] + line)
 
         segments.append((make, stack_ref))
-    weigh(segments, acc_ref, out_ref, None, crosses[0].shape[0], tall)
+    weigh(segments, high_ref, low_ref, out_ref, None, crosses[0].shape[0])
 
 
 def pairs(size, step):
@@ -418,18 +439,19 @@
     own = rows // ntgt
     xst, xop = pl.pallas_call(
         functools.partial(stack_kernel, scale),
-        out_shape=(sds((rows, 2 * dims + 16), BF16), sds((own, depth), BF16)),
+        out_shape=(sds((2 * dims + 16, rows), BF16), sds((own, depth), BF16)),
         out_specs=(VMEM, VMEM),
-        in_specs=[HBM, HBM, VMEM],
+        in_specs=[HBM] * 3,
         scratch_shapes=[
             pltpu.VMEM((dims, rows), F32),
             pltpu.VMEM((dims, own), F32),
             pltpu.VMEM((1, own), jnp.int32),
-            pltpu.SemaphoreType.DMA((3,)),
+            pltpu.VMEM(block_mask.shape, jnp.int32),
+            pltpu.SemaphoreType.DMA((4,)),
         ],
         compiler_params=params(8),
         name="stack",
-    )(in_hbm(source_pca), in_hbm(xl), block_mask)
+    )(in_hbm(source_pca), in_hbm(xl), in_hbm(block_mask))
 
     def rows_parts(value, combine):
         other = swap(value, "tgt", 1)
@@ -477,8 +499,8 @@
         in_specs=[VMEM] * (2 + len(parts)),
         scratch_shapes=[
             pltpu.VMEM((8, rows), F32),
-            pltpu.VMEM((cols, LANES), F32),
-            pltpu.VMEM((min(256, cols), 2 * dims + 16), F32),
+            pltpu.VMEM((2 * dims + 16, min(256, cols)), F32),
+            pltpu.VMEM((dims + 16, min(256, cols)), F32),
         ],
         compiler_params=params(8),
         name="last_col",
@@ -492,7 +514,7 @@
         width = 2 * len(ks) * cols
         own_cross, stack = pl.pallas_call(
             functools.partial(ready_kernel, eps_scale, len(ks), row_lines[0]),
-            out_shape=(pltpu.VMEM((own, width), F32), sds((width, 2 * dims + 16), BF16)),
+            out_shape=(pltpu.VMEM((own, width), F32), sds((2 * dims + 16, width), BF16)),
             out_specs=(VMEM, VMEM),
             in_specs=[VMEM] * (2 + 3 * len(ks)),
             scratch_shapes=[
@@ -515,7 +537,8 @@
         in_specs=[VMEM] * (2 * len(sizes) + len(gs)),
         scratch_shapes=[
             pltpu.VMEM((8, total_cols), F32),
-            pltpu.VMEM((min(256, own), 2 * dims + 16), F32),
+            pltpu.VMEM((2 * dims + 16, min(256, own)), F32),
+            pltpu.VMEM((dims + 16, min(256, own)), F32),
         ],
         compiler_params=params(8),
         name="final",

time: 101 us -> 95.8 us (0.949)
  Pallas kernels: 38.1 us -> 32.2 us
    pallas_call x1, Pallas kernels: 4.91 us -> 2.64 us  [shards(): pl.pallas_call(functools.partial(row_kernel, total_cols, len(parts)), out...]
    pallas_call x4, Pallas kernels: 8.03 us -> 6.41 us  [shards(): pl.pallas_call(functools.partial(ready_kernel, eps_scale, len(ks), row_li...]
    pallas_call x1, Pallas kernels: 7.14 us -> 5.76 us  [shards(): pl.pallas_call(functools.partial(first_kernel, scale, eps_scale), out_sha...]
  transfers between devices with their start and end apart: 28 -> 28, of which waited for: 11 -> 11; matrix products, arithmetic and copies ran while one was open for 1% -> 1% of each run, Pallas kernels for 10% -> 8%
where the time goes in v2:
time: 95.8 us; the launch traced here: 95.6 us
  starting transfers between devices  32.9 us (34%)
  Pallas kernels  32.2 us (34%)
  waiting for transfers between devices  28.8 us (30%)
    ppermute x28, starting transfers between devices, swap(): return lax.ppermute(value, axis, pairs(lax.axis_size(axis), step))  32.9 us
    ppermute x28, waiting for transfers between devices, swap(): return lax.ppermute(value, axis, pairs(lax.axis_size(axis), step))  28.8 us
    pallas_call x4, Pallas kernels, shards(): pl.pallas_call(functools.partial(ready_kernel, eps_scale, len(ks), row_li...  6.41 us
    pallas_call x1, Pallas kernels, shards(): pl.pallas_call(functools.partial(final_kernel, sizes), out_shape=sds((dim...  6.21 us
    pallas_call x1, Pallas kernels, shards(): pl.pallas_call(functools.partial(last_col_kernel, total_rows, len(parts))...  5.82 us
    pallas_call x1, Pallas kernels, shards(): pl.pallas_call(functools.partial(first_kernel, scale, eps_scale), out_sha...  5.76 us
    pallas_call x1, Pallas kernels, shards(): pl.pallas_call(functools.partial(col_kernel, total_rows, len(parts)), out...  3.92 us
    pallas_call x1, Pallas kernels, shards(): pl.pallas_call(functools.partial(row_kernel, total_cols, len(parts)), out...  2.64 us
  transfers between devices with their start and end apart: 28, of which 11 were waited for; matrix products, arithmetic and copies ran while one was open for 1% of the time, Pallas kernels for 8%

profile of v2, /device:TPU:0, one launch (start us, length us, event | category | flops | bytes accessed | tf_op | source)
XLA Modules:
  0.0 95.6 jit_solution(5831454072313706872)
XLA Ops:
  0.6 5.8 %first.1 = (f32[1024,4096]{1,0:T(8,128)S(1)}, f32[40,128]{1,0:T(8,128)S(1)}, f32[32,128]{1,0:T(8,128)S(1)}) custom-call(f32[64,4096]{1,0:T(8,128)} %x_hbm.3, f32[64,1024]{1,0:T(8,128)} %refs_0_.1, s32[1,4096]{1,0:T(1,128)} %bitcast.5, s32[1,1024]{1,0:T(1,128)} %bitcast.9, s32[64,64]{1,0:T(8,128)} %mask_hbm.3), custom_call_target="tpu_custom_call" | custom-call | tf_op jit(solution)/shard_map/first/pallas_call | solution.py:416
  6.4 0.6 collective-permute-start
  7.0 0.8 collective-permute-done
  7.9 3.0 %collective-permute-start.1 = (f32[48,128]{1,0:T(8,128)S(1)}, f32[48,128]{1,0:T(8,128)S(1)}, u32[]{:S(2)}, u32[]{:S(2)}) collective-permute-start(f32[48,128]{1,0:T(8,128)S(1)} %pad_maximum_fusion.refs_0_.refs_2_), channel_id=1, source_target_pairs={{0,2},{1,3},{2,0},{3,1},{4,6},{5,7},{6,4},{7,5},{8,10},{9,11},{10,... | collective-permute-start | bytes 73736 | tf_op jit(solution)/shard_map/ppermute | solution.py:381
  10.8 2.6 %collective-permute-start.2 = (f32[48,128]{1,0:T(8,128)S(1)}, f32[48,128]{1,0:T(8,128)S(1)}, u32[]{:S(2)}, u32[]{:S(2)}) collective-permute-start(f32[48,128]{1,0:T(8,128)S(1)} %pad_maximum_fusion.refs_0_.refs_2_), channel_id=1, source_target_pairs={{0,4},{1,5},{2,6},{3,7},{4,0},{5,1},{6,2},{7,3},{8,12},{9,13},{10,... | collective-permute-start | bytes 73736 | tf_op jit(solution)/shard_map/ppermute | solution.py:381
  13.4 0.0 collective-permute-start.3
  13.4 0.0 collective-permute-done.1.refs_1_.refs_2_
  13.4 2.3 %collective-permute-done.2.refs_2_ = f32[48,128]{1,0:T(8,128)S(1)} collective-permute-done((f32[48,128]{1,0:T(8,128)S(1)}, f32[48,128]{1,0:T(8,128)S(1)}, u32[]{:S(2)}, u32[]{:S(2)}) %collective-permute-start.2) | collective-permute-done | bytes 24608 | tf_op jit(solution)/shard_map/ppermute | solution.py:381
  15.8 3.3 %collective-permute-done.3.refs_3_.refs_2_ = f32[48,128]{1,0:T(8,128)S(1)} collective-permute-done((f32[48,128]{1,0:T(8,128)S(1)}, f32[48,128]{1,0:T(8,128)S(1)}, u32[]{:S(2)}, u32[]{:S(2)}) %collective-permute-start.3) | collective-permute-done | bytes 24608 | tf_op jit(solution)/shard_map/ppermute | solution.py:381
  19.0 3.9 %col.1 = (f32[8,128]{1,0:T(8,128)S(1)}, f32[32,128]{1,0:T(8,128)S(1)}) custom-call(f32[1024,4096]{1,0:T(8,128)S(1)} %get-tuple-element.23.cross_ref, f32[32,128]{1,0:T(8,128)S(1)} %get-tuple-element.24.xsq_ref, f32[48,128]{1,0:T(8,128)S(1)} %pad_maximum_fusion.refs_0_.refs_2_, f32[48,128]{1,0:T(8,128)S(1)} %collective-permute-done.1.refs_1_.refs_2_, ...), custom_call_target="tpu_custom_call" | custom-call | tf_op jit(solution)/shard_map/col/pallas_call | solution.py:470
  23.0 1.5 %collective-permute-start.11 = (f32[8,128]{1,0:T(8,128)S(1)}, f32[8,128]{1,0:T(8,128)S(1)}, u32[]{:S(2)}, u32[]{:S(2)}) collective-permute-start(f32[8,128]{1,0:T(8,128)S(1)} %get-tuple-element.35.refs_0_), channel_id=1, source_target_pairs={{0,8},{8,0},{16,24},{24,16},{1,9},{9,1},{17,25},{25,17},{2,10},{10... | collective-permute-start | bytes 12296 | tf_op jit(solution)/shard_map/ppermute | solution.py:381
  24.5 1.5 %collective-permute-start.12 = (f32[8,128]{1,0:T(8,128)S(1)}, f32[8,128]{1,0:T(8,128)S(1)}, u32[]{:S(2)}, u32[]{:S(2)}) collective-permute-start(f32[8,128]{1,0:T(8,128)S(1)} %get-tuple-element.35.refs_0_), channel_id=1, source_target_pairs={{0,16},{8,24},{16,0},{24,8},{1,17},{9,25},{17,1},{25,9},{2,18},{10... | collective-permute-start | bytes 12296 | tf_op jit(solution)/shard_map/ppermute | solution.py:381
  26.0 0.5 collective-permute-start.13
  26.5 0.1 collective-permute-done.11.refs_1_
  26.6 1.5 %collective-permute-done.12.refs_2_ = f32[8,128]{1,0:T(8,128)S(1)} collective-permute-done((f32[8,128]{1,0:T(8,128)S(1)}, f32[8,128]{1,0:T(8,128)S(1)}, u32[]{:S(2)}, u32[]{:S(2)}) %collective-permute-start.12) | collective-permute-done | bytes 4128 | tf_op jit(solution)/shard_map/ppermute | solution.py:381
  28.1 2.4 %collective-permute-done.13.refs_3_ = f32[8,128]{1,0:T(8,128)S(1)} collective-permute-done((f32[8,128]{1,0:T(8,128)S(1)}, f32[8,128]{1,0:T(8,128)S(1)}, u32[]{:S(2)}, u32[]{:S(2)}) %collective-permute-start.13) | collective-permute-done | bytes 4128 | tf_op jit(solution)/shard_map/ppermute | solution.py:381
  30.5 2.6 %row.1 = (f32[1024,4096]{1,0:T(8,128)S(1)}, f32[32,128]{1,0:T(8,128)S(1)}, f32[8,128]{1,0:T(8,128)S(1)}) custom-call(f32[1024,4096]{1,0:T(8,128)S(1)} %get-tuple-element.23.cross_ref, f32[32,128]{1,0:T(8,128)S(1)} %get-tuple-element.26.pot_ref, f32[8,128]{1,0:T(8,128)S(1)} %get-tuple-element.35.refs_0_, ...), custom_call_target="tpu_custom_call", output_to_operand_aliasing={{0}: (0, {})} | custom-call | tf_op jit(solution)/shard_map/row/pallas_call | solution.py:484
  33.2 0.1 collective-permute-start.14
  33.2 1.2 %collective-permute-done.14 = f32[32,128]{1,0:T(8,128)S(1)} collective-permute-done((f32[32,128]{1,0:T(8,128)S(1)}, f32[32,128]{1,0:T(8,128)S(1)}, u32[]{:S(2)}, u32[]{:S(2)}) %collective-permute-start.14) | collective-permute-done | bytes 16416 | tf_op jit(solution)/shard_map/ppermute | solution.py:381
  34.4 0.0 collective-permute-start.15
  34.4 0.8 collective-permute-start.16
  35.2 3.6 %collective-permute-start.17 = (f32[32,128]{1,0:T(8,128)S(1)}, f32[32,128]{1,0:T(8,128)S(1)}, u32[]{:S(2)}, u32[]{:S(2)}) collective-permute-start(f32[32,128]{1,0:T(8,128)S(1)} %add.30.refs_0_), channel_id=1, source_target_pairs={{0,6},{1,7},{2,4},{3,5},{4,2},{5,3},{6,0},{7,1},{8,14},{9,15},{10,... | collective-permute-start | bytes 49160 | tf_op jit(solution)/shard_map/ppermute | solution.py:381
  38.8 1.5 %stack.13 = (bf16[144,4096]{1,0:T(8,128)(2,1)S(1)}, bf16[512,256]{1,0:T(8,128)(2,1)S(1)}) custom-call(f32[64,4096]{1,0:T(8,128)} %x_hbm.3, s32[1,4096]{1,0:T(1,128)} %bitcast.6, s32[64,64]{1,0:T(8,128)} %mask_hbm.3), custom_call_target="tpu_custom_call" | custom-call | tf_op jit(solution)/shard_map/stack/pallas_call | solution.py:440
  40.3 0.0 collective-permute-done.15.refs_1_
  40.3 0.0 collective-permute-done.16.refs_2_
  40.3 0.4 collective-permute-done.17.refs_3_
  40.8 5.8 %last_col.1 = (f32[8,128]{1,0:T(8,128)S(1)}, f32[64,1024]{1,0:T(8,128)S(1)}) custom-call(f32[1024,4096]{1,0:T(8,128)S(1)} %get-tuple-element.37.plan_ref, bf16[144,4096]{1,0:T(8,128)(2,1)S(1)} %get-tuple-element.38.xst_ref, f32[32,128]{1,0:T(8,128)S(1)} %add.30.refs_0_, f32[32,128]{1,0:T(8,128)S(1)} %collective-permute-done.15.refs_1_, ...), custom_call_target="tpu_custom_call" | custom-call | tf_op jit(solution)/shard_map/last_col/pallas_call | solution.py:495
  46.6 0.6 collective-permute-start.18
  47.2 0.5 collective-permute-start.19
  47.7 2.5 %collective-permute-start.20 = (f32[8,128]{1,0:T(8,128)S(1)}, f32[8,128]{1,0:T(8,128)S(1)}, u32[]{:S(2)}, u32[]{:S(2)}) collective-permute-start(f32[8,128]{1,0:T(8,128)S(1)} %get-tuple-element.40), channel_id=1, source_target_pairs={{0,24},{8,16},{16,8},{24,0},{1,25},{9,17},{17,9},{25,1},{2,26},{10... | collective-permute-start | bytes 12296 | tf_op jit(solution)/shard_map/ppermute | solution.py:381
  50.2 3.6 %collective-permute-start.9 = (f32[64,1024]{1,0:T(8,128)S(1)}, f32[64,1024]{1,0:T(8,128)S(1)}, u32[]{:S(2)}, u32[]{:S(2)}) collective-permute-start(f32[64,1024]{1,0:T(8,128)S(1)} %copy-done), channel_id=1, source_target_pairs={{0,6},{1,7},{2,4},{3,5},{4,2},{5,3},{6,0},{7,1},{8,14},{9,15},{10,... | collective-permute-start | bytes 786440 | tf_op jit(solution)/shard_map/ppermute | solution.py:381
  53.7 0.0 collective-permute-start.7
  53.7 0.0 collective-permute-done.18
  53.7 0.8 collective-permute-start.5
  54.6 0.0 collective-permute-done.19
  54.6 0.0 collective-permute-done.20
  54.6 0.1 collective-permute-start.21
  54.7 0.5 collective-permute-start.4
  55.2 0.7 collective-permute-done.21
  55.8 0.5 collective-permute-start.25
  56.3 4.8 %collective-permute-done.9.refs_0_ = f32[64,1024]{1,0:T(8,128)S(1)} collective-permute-done((f32[64,1024]{1,0:T(8,128)S(1)}, f32[64,1024]{1,0:T(8,128)S(1)}, u32[]{:S(2)}, u32[]{:S(2)}) %collective-permute-start.9) | collective-permute-done | bytes 262176 | tf_op jit(solution)/shard_map/ppermute | solution.py:381
  61.2 0.5 collective-permute-start.26
  61.7 11.2 %collective-permute-done.7.refs_0_ = f32[64,1024]{1,0:T(8,128)S(1)} collective-permute-done((f32[64,1024]{1,0:T(8,128)S(1)}, f32[64,1024]{1,0:T(8,128)S(1)}, u32[]{:S(2)}, u32[]{:S(2)}) %collective-permute-start.7) | collective-permute-done | bytes 262176 | tf_op jit(solution)/shard_map/ppermute | solution.py:381
  72.9 0.5 collective-permute-start.27
  73.4 0.0 collective-permute-done.5.refs_0_
  73.4 0.0 collective-permute-start.10
  73.4 0.0 collective-permute-done.4.refs_1_
  73.4 0.5 collective-permute-start.8
  73.9 0.0 collective-permute-done.25
  73.9 0.1 collective-permute-start.6
  73.9 1.6 %ready.4 = (f32[512,2048]{1,0:T(8,128)S(1)}, bf16[144,2048]{1,0:T(8,128)(2,1)S(1)}) custom-call(bf16[512,256]{1,0:T(8,128)(2,1)S(1)} %get-tuple-element.22.xop_ref, f32[32,128]{1,0:T(8,128)S(1)} %get-tuple-element.26.pot_ref, f32[64,1024]{1,0:T(8,128)S(1)} %copy-done, f32[64,1024]{1,0:T(8,128)S(1)} %collective-permute-done.4.refs_1_, ...), custom_call_target="tpu_custom_call" | custom-call | tf_op jit(solution)/shard_map/ready/pallas_call | solution.py:515
  75.6 0.0 collective-permute-done.26
  75.6 5.8 %collective-permute-start.22 = (f32[2,8,128]{2,1,0:T(8,128)S(1)}, f32[2,8,128]{2,1,0:T(8,128)S(1)}, u32[]{:S(2)}, u32[]{:S(2)}) collective-permute-start(f32[2,8,128]{2,1,0:T(8,128)S(1)} %pad_maximum_fusion.1.refs_8_), channel_id=1, source_target_pairs={{0,2},{1,3},{2,0},{3,1},{4,6},{5,7},{6,4},{7,5},{8,10},{9,11},{10,... | collective-permute-start | bytes 24584 | tf_op jit(solution)/shard_map/ppermute | solution.py:381
  81.4 0.0 collective-permute-done.27
  81.4 0.7 collective-permute-start.23
  82.1 1.6 %collective-permute-start.24 = (f32[2,8,128]{2,1,0:T(8,128)S(1)}, f32[2,8,128]{2,1,0:T(8,128)S(1)}, u32[]{:S(2)}, u32[]{:S(2)}) collective-permute-start(f32[2,8,128]{2,1,0:T(8,128)S(1)} %pad_maximum_fusion.1.refs_8_), channel_id=1, source_target_pairs={{0,6},{1,7},{2,4},{3,5},{4,2},{5,3},{6,0},{7,1},{8,14},{9,15},{10,... | collective-permute-start | bytes 24584 | tf_op jit(solution)/shard_map/ppermute | solution.py:381
  83.7 0.8 add_divide_fusion
  84.5 1.6 %ready.7 = (f32[512,2048]{1,0:T(8,128)S(1)}, bf16[144,2048]{1,0:T(8,128)(2,1)S(1)}) custom-call(bf16[512,256]{1,0:T(8,128)(2,1)S(1)} %get-tuple-element.22.xop_ref, f32[32,128]{1,0:T(8,128)S(1)} %get-tuple-element.26.pot_ref, f32[64,1024]{1,0:T(8,128)S(1)} %collective-permute-done.9.refs_0_, f32[64,1024]{1,0:T(8,128)S(1)} %collective-permute-done.10.refs_1_, ...), custom_call_target="tpu_custom_call" | custom-call | tf_op jit(solution)/shard_map/ready/pallas_call | solution.py:515
  86.1 1.6 %ready.6 = (f32[512,2048]{1,0:T(8,128)S(1)}, bf16[144,2048]{1,0:T(8,128)(2,1)S(1)}) custom-call(bf16[512,256]{1,0:T(8,128)(2,1)S(1)} %get-tuple-element.22.xop_ref, f32[32,128]{1,0:T(8,128)S(1)} %get-tuple-element.26.pot_ref, f32[64,1024]{1,0:T(8,128)S(1)} %collective-permute-done.7.refs_0_, f32[64,1024]{1,0:T(8,128)S(1)} %collective-permute-done.8.refs_1_, ...), custom_call_target="tpu_custom_call" | custom-call | tf_op jit(solution)/shard_map/ready/pallas_call | solution.py:515
  87.8 0.0 collective-permute-done.6.refs_1_
  87.8 1.6 %ready.5 = (f32[512,2048]{1,0:T(8,128)S(1)}, bf16[144,2048]{1,0:T(8,128)(2,1)S(1)}) custom-call(bf16[512,256]{1,0:T(8,128)(2,1)S(1)} %get-tuple-element.22.xop_ref, f32[32,128]{1,0:T(8,128)S(1)} %get-tuple-element.26.pot_ref, f32[64,1024]{1,0:T(8,128)S(1)} %collective-permute-done.5.refs_0_, f32[64,1024]{1,0:T(8,128)S(1)} %collective-permute-done.6.refs_1_, ...), custom_call_target="tpu_custom_call" | custom-call | tf_op jit(solution)/shard_map/ready/pallas_call | solution.py:515
  89.4 0.0 collective-permute-done.22.refs_9_
  89.4 0.0 collective-permute-done.23.refs_10_
  89.4 6.2 %final.1 = f32[64,512]{1,0:T(8,128)} custom-call(f32[512,2048]{1,0:T(8,128)S(1)} %get-tuple-element.27.refs_0_, f32[512,2048]{1,0:T(8,128)S(1)} %get-tuple-element.28.refs_1_, f32[512,2048]{1,0:T(8,128)S(1)} %get-tuple-element.29.refs_2_, f32[512,2048]{1,0:T(8,128)S(1)} %get-tuple-element.30.refs_3_, bf16[144,2048]{1,0:T(8,128)(2,1)S(1)} %get-tuple-element.31.refs_4_, ...), custom_call_target="tpu_custom_call" | custom-call | tf_op jit(solution)/shard_map/final/pallas_call | solution.py:533
  (12 shorter events, 0.1 us)
Async XLA Ops:
  6.4 1.4 %collective-permute-start = (f32[40,128]{1,0:T(8,128)S(1)}, f32[40,128]{1,0:T(8,128)S(1)}, u32[]{:S(2)}, u32[]{:S(2)}) collective-permute-start(f32[40,128]{1,0:T(8,128)S(1)} %get-tuple-element.25), channel_id=1, source_target_pairs={{0,1},{1,0},{2,3},{3,2},{4,5},{5,4},{6,7},{7,6},{8,9},{9,8},{10,11... | collective-permute-start | bytes 61448 | tf_op jit(solution)/shard_map/ppermute | solution.py:381
  7.9 5.6 %collective-permute-start.1 = (f32[48,128]{1,0:T(8,128)S(1)}, f32[48,128]{1,0:T(8,128)S(1)}, u32[]{:S(2)}, u32[]{:S(2)}) collective-permute-start(f32[48,128]{1,0:T(8,128)S(1)} %pad_maximum_fusion.refs_0_.refs_2_), channel_id=1, source_target_pairs={{0,2},{1,3},{2,0},{3,1},{4,6},{5,7},{6,4},{7,5},{8,10},{9,11},{10,... | collective-permute-start | bytes 73736 | tf_op jit(solution)/shard_map/ppermute | solution.py:381
  10.8 4.9 %collective-permute-start.2 = (f32[48,128]{1,0:T(8,128)S(1)}, f32[48,128]{1,0:T(8,128)S(1)}, u32[]{:S(2)}, u32[]{:S(2)}) collective-permute-start(f32[48,128]{1,0:T(8,128)S(1)} %pad_maximum_fusion.refs_0_.refs_2_), channel_id=1, source_target_pairs={{0,4},{1,5},{2,6},{3,7},{4,0},{5,1},{6,2},{7,3},{8,12},{9,13},{10,... | collective-permute-start | bytes 73736 | tf_op jit(solution)/shard_map/ppermute | solution.py:381
  13.4 5.6 %collective-permute-start.3 = (f32[48,128]{1,0:T(8,128)S(1)}, f32[48,128]{1,0:T(8,128)S(1)}, u32[]{:S(2)}, u32[]{:S(2)}) collective-permute-start(f32[48,128]{1,0:T(8,128)S(1)} %pad_maximum_fusion.refs_0_.refs_2_), channel_id=1, source_target_pairs={{0,6},{1,7},{2,4},{3,5},{4,2},{5,3},{6,0},{7,1},{8,14},{9,15},{10,... | collective-permute-start | bytes 73736 | tf_op jit(solution)/shard_map/ppermute | solution.py:381
  23.0 3.7 %collective-permute-start.11 = (f32[8,128]{1,0:T(8,128)S(1)}, f32[8,128]{1,0:T(8,128)S(1)}, u32[]{:S(2)}, u32[]{:S(2)}) collective-permute-start(f32[8,128]{1,0:T(8,128)S(1)} %get-tuple-element.35.refs_0_), channel_id=1, source_target_pairs={{0,8},{8,0},{16,24},{24,16},{1,9},{9,1},{17,25},{25,17},{2,10},{10... | collective-permute-start | bytes 12296 | tf_op jit(solution)/shard_map/ppermute | solution.py:381
  24.5 3.6 %collective-permute-start.12 = (f32[8,128]{1,0:T(8,128)S(1)}, f32[8,128]{1,0:T(8,128)S(1)}, u32[]{:S(2)}, u32[]{:S(2)}) collective-permute-start(f32[8,128]{1,0:T(8,128)S(1)} %get-tuple-element.35.refs_0_), channel_id=1, source_target_pairs={{0,16},{8,24},{16,0},{24,8},{1,17},{9,25},{17,1},{25,9},{2,18},{10... | collective-permute-start | bytes 12296 | tf_op jit(solution)/shard_map/ppermute | solution.py:381
  26.0 4.5 %collective-permute-start.13 = (f32[8,128]{1,0:T(8,128)S(1)}, f32[8,128]{1,0:T(8,128)S(1)}, u32[]{:S(2)}, u32[]{:S(2)}) collective-permute-start(f32[8,128]{1,0:T(8,128)S(1)} %get-tuple-element.35.refs_0_), channel_id=1, source_target_pairs={{0,24},{8,16},{16,8},{24,0},{1,25},{9,17},{17,9},{25,1},{2,26},{10... | collective-permute-start | bytes 12296 | tf_op jit(solution)/shard_map/ppermute | solution.py:381
  33.2 1.2 %collective-permute-start.14 = (f32[32,128]{1,0:T(8,128)S(1)}, f32[32,128]{1,0:T(8,128)S(1)}, u32[]{:S(2)}, u32[]{:S(2)}) collective-permute-start(f32[32,128]{1,0:T(8,128)S(1)} %get-tuple-element.39), channel_id=1, source_target_pairs={{0,1},{1,0},{2,3},{3,2},{4,5},{5,4},{6,7},{7,6},{8,9},{9,8},{10,11... | collective-permute-start | bytes 49160 | tf_op jit(solution)/shard_map/ppermute | solution.py:381
  34.4 5.9 %collective-permute-start.15 = (f32[32,128]{1,0:T(8,128)S(1)}, f32[32,128]{1,0:T(8,128)S(1)}, u32[]{:S(2)}, u32[]{:S(2)}) collective-permute-start(f32[32,128]{1,0:T(8,128)S(1)} %add.30.refs_0_), channel_id=1, source_target_pairs={{0,2},{1,3},{2,0},{3,1},{4,6},{5,7},{6,4},{7,5},{8,10},{9,11},{10,... | collective-permute-start | bytes 49160 | tf_op jit(solution)/shard_map/ppermute | solution.py:381
  34.4 5.9 %collective-permute-start.16 = (f32[32,128]{1,0:T(8,128)S(1)}, f32[32,128]{1,0:T(8,128)S(1)}, u32[]{:S(2)}, u32[]{:S(2)}) collective-permute-start(f32[32,128]{1,0:T(8,128)S(1)} %add.30.refs_0_), channel_id=1, source_target_pairs={{0,4},{1,5},{2,6},{3,7},{4,0},{5,1},{6,2},{7,3},{8,12},{9,13},{10,... | collective-permute-start | bytes 49160 | tf_op jit(solution)/shard_map/ppermute | solution.py:381
  35.2 5.5 %collective-permute-start.17 = (f32[32,128]{1,0:T(8,128)S(1)}, f32[32,128]{1,0:T(8,128)S(1)}, u32[]{:S(2)}, u32[]{:S(2)}) collective-permute-start(f32[32,128]{1,0:T(8,128)S(1)} %add.30.refs_0_), channel_id=1, source_target_pairs={{0,6},{1,7},{2,4},{3,5},{4,2},{5,3},{6,0},{7,1},{8,14},{9,15},{10,... | collective-permute-start | bytes 49160 | tf_op jit(solution)/shard_map/ppermute | solution.py:381
  40.8 9.4 %copy-start = (f32[64,1024]{1,0:T(8,128)S(1)}, f32[64,1024]{1,0:T(8,128)}, u32[]{:S(2)}) copy-start(f32[64,1024]{1,0:T(8,128)} %refs_0_.1) | copy-start | bytes 786436
  46.6 7.1 %collective-permute-start.18 = (f32[8,128]{1,0:T(8,128)S(1)}, f32[8,128]{1,0:T(8,128)S(1)}, u32[]{:S(2)}, u32[]{:S(2)}) collective-permute-start(f32[8,128]{1,0:T(8,128)S(1)} %get-tuple-element.40), channel_id=1, source_target_pairs={{0,8},{8,0},{16,24},{24,16},{1,9},{9,1},{17,25},{25,17},{2,10},{10... | collective-permute-start | bytes 12296 | tf_op jit(solution)/shard_map/ppermute | solution.py:381
  47.2 7.4 %collective-permute-start.19 = (f32[8,128]{1,0:T(8,128)S(1)}, f32[8,128]{1,0:T(8,128)S(1)}, u32[]{:S(2)}, u32[]{:S(2)}) collective-permute-start(f32[8,128]{1,0:T(8,128)S(1)} %get-tuple-element.40), channel_id=1, source_target_pairs={{0,16},{8,24},{16,0},{24,8},{1,17},{9,25},{17,1},{25,9},{2,18},{10... | collective-permute-start | bytes 12296 | tf_op jit(solution)/shard_map/ppermute | solution.py:381
  47.7 6.9 %collective-permute-start.20 = (f32[8,128]{1,0:T(8,128)S(1)}, f32[8,128]{1,0:T(8,128)S(1)}, u32[]{:S(2)}, u32[]{:S(2)}) collective-permute-start(f32[8,128]{1,0:T(8,128)S(1)} %get-tuple-element.40), channel_id=1, source_target_pairs={{0,24},{8,16},{16,8},{24,0},{1,25},{9,17},{17,9},{25,1},{2,26},{10... | collective-permute-start | bytes 12296 | tf_op jit(solution)/shard_map/ppermute | solution.py:381
  50.2 11.0 %collective-permute-start.9 = (f32[64,1024]{1,0:T(8,128)S(1)}, f32[64,1024]{1,0:T(8,128)S(1)}, u32[]{:S(2)}, u32[]{:S(2)}) collective-permute-start(f32[64,1024]{1,0:T(8,128)S(1)} %copy-done), channel_id=1, source_target_pairs={{0,6},{1,7},{2,4},{3,5},{4,2},{5,3},{6,0},{7,1},{8,14},{9,15},{10,... | collective-permute-start | bytes 786440 | tf_op jit(solution)/shard_map/ppermute | solution.py:381
  53.7 19.1 %collective-permute-start.7 = (f32[64,1024]{1,0:T(8,128)S(1)}, f32[64,1024]{1,0:T(8,128)S(1)}, u32[]{:S(2)}, u32[]{:S(2)}) collective-permute-start(f32[64,1024]{1,0:T(8,128)S(1)} %copy-done), channel_id=1, source_target_pairs={{0,4},{1,5},{2,6},{3,7},{4,0},{5,1},{6,2},{7,3},{8,12},{9,13},{10,... | collective-permute-start | bytes 786440 | tf_op jit(solution)/shard_map/ppermute | solution.py:381
  53.7 19.6 %collective-permute-start.5 = (f32[64,1024]{1,0:T(8,128)S(1)}, f32[64,1024]{1,0:T(8,128)S(1)}, u32[]{:S(2)}, u32[]{:S(2)}) collective-permute-start(f32[64,1024]{1,0:T(8,128)S(1)} %copy-done), channel_id=1, source_target_pairs={{0,2},{1,3},{2,0},{3,1},{4,6},{5,7},{6,4},{7,5},{8,10},{9,11},{10,... | collective-permute-start | bytes 786440 | tf_op jit(solution)/shard_map/ppermute | solution.py:381
  54.6 1.2 %collective-permute-start.21 = (f32[8,128]{1,0:T(8,128)S(1)}, f32[8,128]{1,0:T(8,128)S(1)}, u32[]{:S(2)}, u32[]{:S(2)}) collective-permute-start(f32[8,128]{1,0:T(8,128)S(1)} %get-tuple-element.42), channel_id=1, source_target_pairs={{0,1},{1,0},{2,3},{3,2},{4,5},{5,4},{6,7},{7,6},{8,9},{9,8},{10,11... | collective-permute-start | bytes 12296 | tf_op jit(solution)/shard_map/ppermute | solution.py:381
  54.7 18.7 %collective-permute-start.4 = (f32[64,1024]{1,0:T(8,128)S(1)}, f32[64,1024]{1,0:T(8,128)S(1)}, u32[]{:S(2)}, u32[]{:S(2)}) collective-permute-start(f32[64,1024]{1,0:T(8,128)S(1)} %copy-done), channel_id=1, source_target_pairs={{0,1},{1,0},{2,3},{3,2},{4,5},{5,4},{6,7},{7,6},{8,9},{9,8},{10,11... | collective-permute-start | bytes 786440 | tf_op jit(solution)/shard_map/ppermute | solution.py:381
  55.8 18.1 %collective-permute-start.25 = (f32[64,1024]{1,0:T(8,128)S(1)}, f32[64,1024]{1,0:T(8,128)S(1)}, u32[]{:S(2)}, u32[]{:S(2)}) collective-permute-start(f32[64,1024]{1,0:T(8,128)S(1)} %get-tuple-element.41), channel_id=1, source_target_pairs={{0,8},{8,0},{16,24},{24,16},{1,9},{9,1},{17,25},{25,17},{2,10},{10... | collective-permute-start | bytes 786440 | tf_op jit(solution)/shard_map/ppermute | solution.py:381
  61.2 14.4 %collective-permute-start.26 = (f32[64,1024]{1,0:T(8,128)S(1)}, f32[64,1024]{1,0:T(8,128)S(1)}, u32[]{:S(2)}, u32[]{:S(2)}) collective-permute-start(f32[64,1024]{1,0:T(8,128)S(1)} %get-tuple-element.41), channel_id=1, source_target_pairs={{0,16},{8,24},{16,0},{24,8},{1,17},{9,25},{17,1},{25,9},{2,18},{10... | collective-permute-start | bytes 786440 | tf_op jit(solution)/shard_map/ppermute | solution.py:381
  72.9 8.5 %collective-permute-start.27 = (f32[64,1024]{1,0:T(8,128)S(1)}, f32[64,1024]{1,0:T(8,128)S(1)}, u32[]{:S(2)}, u32[]{:S(2)}) collective-permute-start(f32[64,1024]{1,0:T(8,128)S(1)} %get-tuple-element.41), channel_id=1, source_target_pairs={{0,24},{8,16},{16,8},{24,0},{1,25},{9,17},{17,9},{25,1},{2,26},{10... | collective-permute-start | bytes 786440 | tf_op jit(solution)/shard_map/ppermute | solution.py:381
  73.4 8.8 %collective-permute-start.10 = (f32[64,1024]{1,0:T(8,128)S(1)}, f32[64,1024]{1,0:T(8,128)S(1)}, u32[]{:S(2)}, u32[]{:S(2)}) collective-permute-start(f32[64,1024]{1,0:T(8,128)S(1)} %collective-permute-done.9.refs_0_), channel_id=1, source_target_pairs={{0,1},{1,0},{2,3},{3,2},{4,5},{5,4},{6,7},{7,6},{8,9},{9,8},{10,11... | collective-permute-start | bytes 786440 | tf_op jit(solution)/shard_map/ppermute | solution.py:381
  73.4 12.8 %collective-permute-start.8 = (f32[64,1024]{1,0:T(8,128)S(1)}, f32[64,1024]{1,0:T(8,128)S(1)}, u32[]{:S(2)}, u32[]{:S(2)}) collective-permute-start(f32[64,1024]{1,0:T(8,128)S(1)} %collective-permute-done.7.refs_0_), channel_id=1, source_target_pairs={{0,1},{1,0},{2,3},{3,2},{4,5},{5,4},{6,7},{7,6},{8,9},{9,8},{10,11... | collective-permute-start | bytes 786440 | tf_op jit(solution)/shard_map/ppermute | solution.py:381
  73.9 13.9 %collective-permute-start.6 = (f32[64,1024]{1,0:T(8,128)S(1)}, f32[64,1024]{1,0:T(8,128)S(1)}, u32[]{:S(2)}, u32[]{:S(2)}) collective-permute-start(f32[64,1024]{1,0:T(8,128)S(1)} %collective-permute-done.5.refs_0_), channel_id=1, source_target_pairs={{0,1},{1,0},{2,3},{3,2},{4,5},{5,4},{6,7},{7,6},{8,9},{9,8},{10,11... | collective-permute-start | bytes 786440 | tf_op jit(solution)/shard_map/ppermute | solution.py:381
  75.6 13.8 %collective-permute-start.22 = (f32[2,8,128]{2,1,0:T(8,128)S(1)}, f32[2,8,128]{2,1,0:T(8,128)S(1)}, u32[]{:S(2)}, u32[]{:S(2)}) collective-permute-start(f32[2,8,128]{2,1,0:T(8,128)S(1)} %pad_maximum_fusion.1.refs_8_), channel_id=1, source_target_pairs={{0,2},{1,3},{2,0},{3,1},{4,6},{5,7},{6,4},{7,5},{8,10},{9,11},{10,... | collective-permute-start | bytes 24584 | tf_op jit(solution)/shard_map/ppermute | solution.py:381
  81.4 8.0 %collective-permute-start.23 = (f32[2,8,128]{2,1,0:T(8,128)S(1)}, f32[2,8,128]{2,1,0:T(8,128)S(1)}, u32[]{:S(2)}, u32[]{:S(2)}) collective-permute-start(f32[2,8,128]{2,1,0:T(8,128)S(1)} %pad_maximum_fusion.1.refs_8_), channel_id=1, source_target_pairs={{0,4},{1,5},{2,6},{3,7},{4,0},{5,1},{6,2},{7,3},{8,12},{9,13},{10,... | collective-permute-start | bytes 24584 | tf_op jit(solution)/shard_map/ppermute | solution.py:381
  82.1 7.3 %collective-permute-start.24 = (f32[2,8,128]{2,1,0:T(8,128)S(1)}, f32[2,8,128]{2,1,0:T(8,128)S(1)}, u32[]{:S(2)}, u32[]{:S(2)}) collective-permute-start(f32[2,8,128]{2,1,0:T(8,128)S(1)} %pad_maximum_fusion.1.refs_8_), channel_id=1, source_target_pairs={{0,6},{1,7},{2,4},{3,5},{4,2},{5,3},{6,0},{7,1},{8,14},{9,15},{10,... | collective-permute-start | bytes 24584 | tf_op jit(solution)/shard_map/ppermute | solution.py:381

commit v3 on v2

--- a/solution.py
+++ b/solution.py
@@ -271,7 +271,7 @@
 def stack_kernel(
     scale, x_hbm, sl_hbm, mask_hbm, xst_ref, xop_ref, x_ref, own_ref, sl_ref, mask_ref, sems
 ):
-    own, rows = xop_ref.shape[0], x_ref.shape[1]
+    own, rows = xop_ref.shape[1], x_ref.shape[1]
     start = pl.multiple_of(lax.axis_index("tgt") * own, own)
     mine = pl.ds(start, own)
     copies = fetch(
@@ -288,8 +288,7 @@
         copy.wait()
     high, low = halves(own_ref[...] * scale)
     barred = barred_by(mask_ref, onehot(sl_ref[...], clusters), True)
-    stacked = jnp.concatenate([high.astype(F32), low.astype(F32), high.astype(F32), barred], 0)
-    xop_ref[...] = stacked.T.astype(BF16)
+    xop_ref[...] = jnp.concatenate([high, low, high, barred.astype(BF16)], 0)
     copies[3].wait()
     step = min(512, rows)
     for k in range(0, rows, step):
@@ -312,65 +311,84 @@
 
 def ready_kernel(eps_scale, n_near, lines, xop_ref, pot_ref, *refs):
     near, far, labels = refs[:n_near], refs[n_near : 2 * n_near], refs[2 * n_near : 3 * n_near]
-    cross_ref, yst_ref, yop_ref, ysq_ref, shift_ref = refs[3 * n_near :]
-    own, total = cross_ref.shape
+    cross_ref, yst_ref, square_ref, yop_ref = refs[3 * n_near :]
+    total, own = cross_ref.shape
     dims, cols = near[0].shape
-    clusters = yop_ref.shape[0] - 3 * dims
+    clusters = yop_ref.shape[1] - 3 * dims
     tiles = cols // LANES
-    place = lax.axis_index("tgt")
-    spread_lanes(shift_ref, pot_ref[pl.ds(place * (own // LANES), own // LANES), :])
     for n, ref in enumerate(near + far):
         at = slice(n * cols, (n + 1) * cols)
         y = ref[...]
         high, low = halves(y)
         stack_lines(yst_ref, at, high, low)
-        yop_ref[: 3 * dims, at] = jnp.concatenate([high, high, low], 0)
         side, which = divmod(n, n_near)
+        hots = []
         for k in range(tiles):
             line = lines + side * tiles + k
-            lanes = slice(n * cols + k * LANES, n * cols + (k + 1) * LANES)
             label = labels[which][line : line + 1, :].astype(jnp.int32)
-            yop_ref[3 * dims :, lanes] = onehot(label, clusters).astype(BF16)
-        ysq = jnp.sum(y * y, 0, keepdims=True) * (-eps_scale)
-        ysq_ref[:, at] = jnp.broadcast_to(ysq, (8, cols))
-    width = min(1024, total)
+            hots.append(onehot(label, clusters).astype(F32))
+        ysq = jnp.sum(y * y, 0, keepdims=True) * eps_scale
+        for k in range(tiles):
+            square_ref[n * tiles + k : n * tiles + k + 1, :] = ysq[:, k * LANES : (k + 1) * LANES]
+        high, low = high.astype(F32), low.astype(F32)
+        stacked = jnp.concatenate([high, high, low, jnp.concatenate(hots, 1)], 0)
+        yop_ref[at, :] = stacked.T.astype(BF16)
+    place = lax.axis_index("tgt") * (own // LANES)
+    pots = [pot_ref[pl.ds(place + p, 1), :] for p in range(own // LANES)]
+    tall = min(1024, total)
 
     def fill(q, unused):
-        at = pl.multiple_of(q * width, width)
-        cross = jnp.dot(xop_ref[...], yop_ref[:, pl.ds(at, width)], preferred_element_type=F32)
-        for p in range(width // LANES):
-            here = pl.ds(at + p * LANES, LANES)
-            line = jnp.broadcast_to(ysq_ref[0:1, here], (own, LANES))
-            cross_ref[:, here] = cross[:, p * LANES : (p + 1) * LANES] + (shift_ref[...] + line)
+        here = pl.ds(pl.multiple_of(q * tall, tall), tall)
+        cross = jnp.dot(yop_ref[here, :], xop_ref[...], preferred_element_type=F32)
+        for p in range(own // LANES):
+            lanes = slice(p * LANES, (p + 1) * LANES)
+            cross_ref[here, lanes] = cross[:, lanes] + jnp.broadcast_to(pots[p], (tall, LANES))
         return unused
 
-    lax.fori_loop(0, total // width, fill, 0)
+    lax.fori_loop(0, total // tall, fill, 0)
 
 
 def final_kernel(sizes, *refs):
     n = len(sizes)
-    crosses, stacks, gs = refs[:n], refs[n : 2 * n], refs[2 * n : -4]
-    out_ref, shift_ref, high_ref, low_ref = refs[-4:]
-    tall = high_ref.shape[1]
-    segments = []
-    col = first = 0
-    for size, cross_ref, stack_ref in zip(sizes, crosses, stacks):
-        base = col
-        for side in range(2):
-            for g in gs[first : first + size]:
-                for k in range(g.shape[1]):
-                    shift_ref[:, col : col + LANES] = jnp.broadcast_to(
-                        g[side, k : k + 1, :], (8, LANES)
-                    )
-                    col += LANES
-        first += size
-
-        def make(span, k, cross_ref=cross_ref, base=base):
-            line = jnp.broadcast_to(shift_ref[0:1, base + k : base + k + LANES], (tall, LANES))
-            return jnp.exp2(cross_ref[span, k : k + LANES] + line)
-
-        segments.append((make, stack_ref))
-    weigh(segments, high_ref, low_ref, out_ref, None, crosses[0].shape[0])
+    crosses, stacks, squares, gs = refs[:n], refs[n : 2 * n], refs[2 * n : 3 * n], refs[3 * n : -3]
+    out_ref, high_ref, low_ref = refs[-3:]
+    dims, own = out_ref.shape
+    short = low_ref.shape[0]
+    first, base = True, 0
+    for size, cross_ref, stack_ref, square_ref in zip(sizes, crosses, stacks, squares):
+        g = [
+            ref[side, k : k + 1, :]
+            for side in range(2)
+            for ref in gs[base : base + size]
+            for k in range(ref.shape[1])
+        ]
+        base += size
+        deep = min(1024, cross_ref.shape[0])
+        for c in range(0, cross_ref.shape[0], deep):
+            highs, lows = [], []
+            for r in range(c, c + deep, LANES):
+                k = r // LANES
+                line = g[k] - square_ref[k : k + 1, :]
+                shift = jnp.broadcast_to(line, (LANES, LANES)).T
+                parts = [
+                    halves(jnp.exp2(cross_ref[r : r + LANES, p : p + LANES] + shift))
+                    for p in range(0, own, LANES)
+                ]
+                highs.append(jnp.concatenate([part[0] for part in parts], 1))
+                lows.append(jnp.concatenate([part[1] for part in parts], 1))
+            stack = stack_ref[:, c : c + deep]
+            with_high = jnp.dot(stack, jnp.concatenate(highs, 0), preferred_element_type=F32)
+            with_low = jnp.dot(stack[:short], jnp.concatenate(lows, 0), preferred_element_type=F32)
+            if first:
+                high_ref[...] = with_high
+                low_ref[...] = with_low
+            else:
+                high_ref[...] += with_high
+                low_ref[...] += with_low
+            first = False
+    mass = high_ref[dims : dims + 1, :] + low_ref[dims : dims + 1, :]
+    weight = (high_ref[:dims, :] + low_ref[:dims, :]) + high_ref[short:, :]
+    out_ref[...] = weight / mass
 
 
 def pairs(size, step):
@@ -439,7 +457,7 @@
     own = rows // ntgt
     xst, xop = pl.pallas_call(
         functools.partial(stack_kernel, scale),
-        out_shape=(sds((2 * dims + 16, rows), BF16), sds((own, depth), BF16)),
+        out_shape=(sds((2 * dims + 16, rows), BF16), sds((depth, own), BF16)),
         out_specs=(VMEM, VMEM),
         in_specs=[HBM] * 3,
         scratch_shapes=[
@@ -506,27 +524,29 @@
         name="last_col",
     )(in_vmem(plan), xst, *parts)
     mass = add(cols_parts(mass))
-    weights = [weight] + [swap(weight, "src", k) for k in range(1, nsrc)]
+    weights = [weight] + [swap(weight, "src", k) for k in range(1, nsrc - 1)]
+    weights.append(swap(weight, "src", nsrc - 1))
     pot = g - math.log2(total_cols) - jnp.log2(mass)
 
-    crosses, stacks, sizes = [], [], [len(ks) for ks in legs]
+    crosses, stacks, squares, sizes = [], [], [], [len(ks) for ks in legs]
     for leg, ks in enumerate(legs):
         width = 2 * len(ks) * cols
-        own_cross, stack = pl.pallas_call(
+        own_cross, stack, square = pl.pallas_call(
             functools.partial(ready_kernel, eps_scale, len(ks), row_lines[0]),
-            out_shape=(pltpu.VMEM((own, width), F32), sds((2 * dims + 16, width), BF16)),
-            out_specs=(VMEM, VMEM),
+            out_shape=(
+                pltpu.VMEM((width, own), F32),
+                sds((2 * dims + 16, width), BF16),
+                sds((width // LANES, LANES), F32),
+            ),
+            out_specs=(VMEM,) * 3,
             in_specs=[VMEM] * (2 + 3 * len(ks)),
-            scratch_shapes=[
-                pltpu.VMEM((depth, width), BF16),
-                pltpu.VMEM((8, width), F32),
-                pltpu.VMEM((own, LANES), F32),
-            ],
-            compiler_params=params(4 + (width * (2 * depth + 32) >> 20)),
+            scratch_shapes=[pltpu.VMEM((width, depth), BF16)],
+            compiler_params=params(6 + (width * 2 * depth >> 20)),
             name="ready",
         )(xop, pots, *near[leg], *far[leg], *[labelled[k] for k in ks])
         crosses.append(in_vmem(own_cross))
         stacks.append(stack)
+        squares.append(square)
 
     both = jnp.stack([pot, swap(pot, "tgt", 1)])
     gs = [both] + [swap(both, "tgt", k) for k in range(2, ntgt, 2)]
@@ -534,15 +554,11 @@
         functools.partial(final_kernel, sizes),
         out_shape=sds((dims, own), F32),
         out_specs=VMEM,
-        in_specs=[VMEM] * (2 * len(sizes) + len(gs)),
-        scratch_shapes=[
-            pltpu.VMEM((8, total_cols), F32),
-            pltpu.VMEM((2 * dims + 16, min(256, own)), F32),
-            pltpu.VMEM((dims + 16, min(256, own)), F32),
-        ],
+        in_specs=[VMEM] * (3 * len(sizes) + len(gs)),
+        scratch_shapes=[pltpu.VMEM((2 * dims + 16, own), F32), pltpu.VMEM((dims + 16, own), F32)],
         compiler_params=params(8),
         name="final",
-    )(*crosses, *stacks, *gs)
+    )(*crosses, *stacks, *squares, *gs)
     target_projection = add(weights) / mass.reshape(1, cols)
     return (source_projection, target_projection)
 

time: 95.8 us -> 94.9 us (level)
  Pallas kernels: 32.2 us -> 31 us
    pallas_call x4, Pallas kernels: 6.41 us -> 5.18 us  [shards(): pl.pallas_call(functools.partial(ready_kernel, eps_scale, len(ks), row_li...]
  transfers between devices with their start and end apart: 28 -> 28, of which waited for: 11 -> 11; matrix products, arithmetic and copies ran while one was open for 1% -> 1% of each run, Pallas kernels for 8% -> 7%
where the time goes in v3:
time: 94.9 us; the launch traced here: 94.7 us
  starting transfers between devices  33.2 us (35%)
  Pallas kernels  31 us (33%)
  waiting for transfers between devices  28.8 us (30%)
    ppermute x28, starting transfers between devices, swap(): return lax.ppermute(value, axis, pairs(lax.axis_size(axis), step))  33.2 us
    ppermute x28, waiting for transfers between devices, swap(): return lax.ppermute(value, axis, pairs(lax.axis_size(axis), step))  28.8 us
    pallas_call x1, Pallas kernels, shards(): pl.pallas_call(functools.partial(final_kernel, sizes), out_shape=sds((dim...  6.2 us
    pallas_call x1, Pallas kernels, shards(): pl.pallas_call(functools.partial(last_col_kernel, total_rows, len(parts))...  5.82 us
    pallas_call x1, Pallas kernels, shards(): pl.pallas_call(functools.partial(first_kernel, scale, eps_scale), out_sha...  5.76 us
    pallas_call x4, Pallas kernels, shards(): pl.pallas_call(functools.partial(ready_kernel, eps_scale, len(ks), row_li...  5.18 us
    pallas_call x1, Pallas kernels, shards(): pl.pallas_call(functools.partial(col_kernel, total_rows, len(parts)), out...  3.92 us
    pallas_call x1, Pallas kernels, shards(): pl.pallas_call(functools.partial(row_kernel, total_cols, len(parts)), out...  2.64 us
  transfers between devices with their start and end apart: 28, of which 11 were waited for; matrix products, arithmetic and copies ran while one was open for 1% of the time, Pallas kernels for 7%

profile of v3, /device:TPU:0, one launch (start us, length us, event | category | flops | bytes accessed | tf_op | source)
XLA Modules:
  0.0 94.7 jit_solution(2361799705899884505)
XLA Ops:
  0.6 5.8 %first.1 = (f32[1024,4096]{1,0:T(8,128)S(1)}, f32[40,128]{1,0:T(8,128)S(1)}, f32[32,128]{1,0:T(8,128)S(1)}) custom-call(f32[64,4096]{1,0:T(8,128)} %x_hbm.3, f32[64,1024]{1,0:T(8,128)} %refs_0_.1, s32[1,4096]{1,0:T(1,128)} %bitcast.5, s32[1,1024]{1,0:T(1,128)} %bitcast.9, s32[64,64]{1,0:T(8,128)} %mask_hbm.3), custom_call_target="tpu_custom_call" | custom-call | tf_op jit(solution)/shard_map/first/pallas_call | solution.py:434
  6.4 0.6 collective-permute-start
  7.0 0.8 collective-permute-done
  7.8 3.0 %collective-permute-start.1 = (f32[48,128]{1,0:T(8,128)S(1)}, f32[48,128]{1,0:T(8,128)S(1)}, u32[]{:S(2)}, u32[]{:S(2)}) collective-permute-start(f32[48,128]{1,0:T(8,128)S(1)} %pad_maximum_fusion.refs_0_.refs_2_), channel_id=1, source_target_pairs={{0,2},{1,3},{2,0},{3,1},{4,6},{5,7},{6,4},{7,5},{8,10},{9,11},{10,... | collective-permute-start | bytes 73736 | tf_op jit(solution)/shard_map/ppermute | solution.py:399
  10.8 2.6 %collective-permute-start.2 = (f32[48,128]{1,0:T(8,128)S(1)}, f32[48,128]{1,0:T(8,128)S(1)}, u32[]{:S(2)}, u32[]{:S(2)}) collective-permute-start(f32[48,128]{1,0:T(8,128)S(1)} %pad_maximum_fusion.refs_0_.refs_2_), channel_id=1, source_target_pairs={{0,4},{1,5},{2,6},{3,7},{4,0},{5,1},{6,2},{7,3},{8,12},{9,13},{10,... | collective-permute-start | bytes 73736 | tf_op jit(solution)/shard_map/ppermute | solution.py:399
  13.4 0.0 collective-permute-start.3
  13.4 0.0 collective-permute-done.1.refs_1_.refs_2_
  13.4 2.3 %collective-permute-done.2.refs_2_ = f32[48,128]{1,0:T(8,128)S(1)} collective-permute-done((f32[48,128]{1,0:T(8,128)S(1)}, f32[48,128]{1,0:T(8,128)S(1)}, u32[]{:S(2)}, u32[]{:S(2)}) %collective-permute-start.2) | collective-permute-done | bytes 24608 | tf_op jit(solution)/shard_map/ppermute | solution.py:399
  15.7 3.3 %collective-permute-done.3.refs_3_.refs_2_ = f32[48,128]{1,0:T(8,128)S(1)} collective-permute-done((f32[48,128]{1,0:T(8,128)S(1)}, f32[48,128]{1,0:T(8,128)S(1)}, u32[]{:S(2)}, u32[]{:S(2)}) %collective-permute-start.3) | collective-permute-done | bytes 24608 | tf_op jit(solution)/shard_map/ppermute | solution.py:399
  19.0 3.9 %col.1 = (f32[8,128]{1,0:T(8,128)S(1)}, f32[32,128]{1,0:T(8,128)S(1)}) custom-call(f32[1024,4096]{1,0:T(8,128)S(1)} %get-tuple-element.27.cross_ref, f32[32,128]{1,0:T(8,128)S(1)} %get-tuple-element.28.xsq_ref, f32[48,128]{1,0:T(8,128)S(1)} %pad_maximum_fusion.refs_0_.refs_2_, f32[48,128]{1,0:T(8,128)S(1)} %collective-permute-done.1.refs_1_.refs_2_, ...), custom_call_target="tpu_custom_call" | custom-call | tf_op jit(solution)/shard_map/col/pallas_call | solution.py:488
  23.0 1.5 %collective-permute-start.11 = (f32[8,128]{1,0:T(8,128)S(1)}, f32[8,128]{1,0:T(8,128)S(1)}, u32[]{:S(2)}, u32[]{:S(2)}) collective-permute-start(f32[8,128]{1,0:T(8,128)S(1)} %get-tuple-element.43.refs_0_), channel_id=1, source_target_pairs={{0,8},{8,0},{16,24},{24,16},{1,9},{9,1},{17,25},{25,17},{2,10},{10... | collective-permute-start | bytes 12296 | tf_op jit(solution)/shard_map/ppermute | solution.py:399
  24.5 1.5 %collective-permute-start.12 = (f32[8,128]{1,0:T(8,128)S(1)}, f32[8,128]{1,0:T(8,128)S(1)}, u32[]{:S(2)}, u32[]{:S(2)}) collective-permute-start(f32[8,128]{1,0:T(8,128)S(1)} %get-tuple-element.43.refs_0_), channel_id=1, source_target_pairs={{0,16},{8,24},{16,0},{24,8},{1,17},{9,25},{17,1},{25,9},{2,18},{10... | collective-permute-start | bytes 12296 | tf_op jit(solution)/shard_map/ppermute | solution.py:399
  26.0 0.5 collective-permute-start.13
  26.5 0.1 collective-permute-done.11.refs_1_
  26.6 1.5 %collective-permute-done.12.refs_2_ = f32[8,128]{1,0:T(8,128)S(1)} collective-permute-done((f32[8,128]{1,0:T(8,128)S(1)}, f32[8,128]{1,0:T(8,128)S(1)}, u32[]{:S(2)}, u32[]{:S(2)}) %collective-permute-start.12) | collective-permute-done | bytes 4128 | tf_op jit(solution)/shard_map/ppermute | solution.py:399
  28.1 2.4 %collective-permute-done.13.refs_3_ = f32[8,128]{1,0:T(8,128)S(1)} collective-permute-done((f32[8,128]{1,0:T(8,128)S(1)}, f32[8,128]{1,0:T(8,128)S(1)}, u32[]{:S(2)}, u32[]{:S(2)}) %collective-permute-start.13) | collective-permute-done | bytes 4128 | tf_op jit(solution)/shard_map/ppermute | solution.py:399
  30.5 2.6 %row.1 = (f32[1024,4096]{1,0:T(8,128)S(1)}, f32[32,128]{1,0:T(8,128)S(1)}, f32[8,128]{1,0:T(8,128)S(1)}) custom-call(f32[1024,4096]{1,0:T(8,128)S(1)} %get-tuple-element.27.cross_ref, f32[32,128]{1,0:T(8,128)S(1)} %get-tuple-element.30.pot_ref, f32[8,128]{1,0:T(8,128)S(1)} %get-tuple-element.43.refs_0_, ...), custom_call_target="tpu_custom_call", output_to_operand_aliasing={{0}: (0, {})} | custom-call | tf_op jit(solution)/shard_map/row/pallas_call | solution.py:502
  33.2 0.1 collective-permute-start.14
  33.3 1.2 %collective-permute-done.14 = f32[32,128]{1,0:T(8,128)S(1)} collective-permute-done((f32[32,128]{1,0:T(8,128)S(1)}, f32[32,128]{1,0:T(8,128)S(1)}, u32[]{:S(2)}, u32[]{:S(2)}) %collective-permute-start.14) | collective-permute-done | bytes 16416 | tf_op jit(solution)/shard_map/ppermute | solution.py:399
  34.4 0.0 collective-permute-start.15
  34.4 0.8 collective-permute-start.16
  35.3 3.6 %collective-permute-start.17 = (f32[32,128]{1,0:T(8,128)S(1)}, f32[32,128]{1,0:T(8,128)S(1)}, u32[]{:S(2)}, u32[]{:S(2)}) collective-permute-start(f32[32,128]{1,0:T(8,128)S(1)} %add.30.refs_0_), channel_id=1, source_target_pairs={{0,6},{1,7},{2,4},{3,5},{4,2},{5,3},{6,0},{7,1},{8,14},{9,15},{10,... | collective-permute-start | bytes 49160 | tf_op jit(solution)/shard_map/ppermute | solution.py:399
  38.8 1.5 %stack.13 = (bf16[144,4096]{1,0:T(8,128)(2,1)S(1)}, bf16[256,512]{1,0:T(8,128)(2,1)S(1)}) custom-call(f32[64,4096]{1,0:T(8,128)} %x_hbm.3, s32[1,4096]{1,0:T(1,128)} %bitcast.6, s32[64,64]{1,0:T(8,128)} %mask_hbm.3), custom_call_target="tpu_custom_call" | custom-call | tf_op jit(solution)/shard_map/stack/pallas_call | solution.py:458
  40.3 0.0 collective-permute-done.15.refs_1_
  40.3 0.0 collective-permute-done.16.refs_2_
  40.3 0.4 collective-permute-done.17.refs_3_
  40.8 5.8 %last_col.1 = (f32[8,128]{1,0:T(8,128)S(1)}, f32[64,1024]{1,0:T(8,128)S(1)}) custom-call(f32[1024,4096]{1,0:T(8,128)S(1)} %get-tuple-element.45.plan_ref, bf16[144,4096]{1,0:T(8,128)(2,1)S(1)} %get-tuple-element.46.xst_ref, f32[32,128]{1,0:T(8,128)S(1)} %add.30.refs_0_, f32[32,128]{1,0:T(8,128)S(1)} %collective-permute-done.15.refs_1_, ...), custom_call_target="tpu_custom_call" | custom-call | tf_op jit(solution)/shard_map/last_col/pallas_call | solution.py:513
  46.6 0.6 collective-permute-start.18
  47.2 0.5 collective-permute-start.19
  47.7 2.5 %collective-permute-start.20 = (f32[8,128]{1,0:T(8,128)S(1)}, f32[8,128]{1,0:T(8,128)S(1)}, u32[]{:S(2)}, u32[]{:S(2)}) collective-permute-start(f32[8,128]{1,0:T(8,128)S(1)} %get-tuple-element.48), channel_id=1, source_target_pairs={{0,24},{8,16},{16,8},{24,0},{1,25},{9,17},{17,9},{25,1},{2,26},{10... | collective-permute-start | bytes 12296 | tf_op jit(solution)/shard_map/ppermute | solution.py:399
  50.2 3.6 %collective-permute-start.9 = (f32[64,1024]{1,0:T(8,128)S(1)}, f32[64,1024]{1,0:T(8,128)S(1)}, u32[]{:S(2)}, u32[]{:S(2)}) collective-permute-start(f32[64,1024]{1,0:T(8,128)S(1)} %copy-done), channel_id=1, source_target_pairs={{0,6},{1,7},{2,4},{3,5},{4,2},{5,3},{6,0},{7,1},{8,14},{9,15},{10,... | collective-permute-start | bytes 786440 | tf_op jit(solution)/shard_map/ppermute | solution.py:399
  53.7 0.0 collective-permute-start.7
  53.7 0.0 collective-permute-done.18
  53.7 0.8 collective-permute-start.5
  54.6 0.0 collective-permute-done.19
  54.6 0.0 collective-permute-done.20
  54.6 0.1 collective-permute-start.21
  54.7 0.5 collective-permute-start.4
  55.2 0.7 collective-permute-done.21
  55.8 0.5 collective-permute-start.25
  56.3 4.9 %collective-permute-done.9.refs_0_ = f32[64,1024]{1,0:T(8,128)S(1)} collective-permute-done((f32[64,1024]{1,0:T(8,128)S(1)}, f32[64,1024]{1,0:T(8,128)S(1)}, u32[]{:S(2)}, u32[]{:S(2)}) %collective-permute-start.9) | collective-permute-done | bytes 262176 | tf_op jit(solution)/shard_map/ppermute | solution.py:399
  61.2 0.5 collective-permute-start.26
  61.7 11.2 %collective-permute-done.7.refs_0_ = f32[64,1024]{1,0:T(8,128)S(1)} collective-permute-done((f32[64,1024]{1,0:T(8,128)S(1)}, f32[64,1024]{1,0:T(8,128)S(1)}, u32[]{:S(2)}, u32[]{:S(2)}) %collective-permute-start.7) | collective-permute-done | bytes 262176 | tf_op jit(solution)/shard_map/ppermute | solution.py:399
  72.9 0.5 collective-permute-start.27
  73.3 0.0 collective-permute-done.5.refs_0_
  73.3 0.0 collective-permute-start.10
  73.3 0.0 collective-permute-done.4.refs_1_
  73.4 0.5 collective-permute-start.8
  73.9 0.0 collective-permute-done.25
  73.9 0.1 collective-permute-start.6
  73.9 1.3 %ready.4 = (f32[2048,512]{1,0:T(8,128)S(1)}, bf16[144,2048]{1,0:T(8,128)(2,1)S(1)}, f32[16,128]{1,0:T(8,128)S(1)}) custom-call(bf16[256,512]{1,0:T(8,128)(2,1)S(1)} %get-tuple-element.26.xop_ref, f32[32,128]{1,0:T(8,128)S(1)} %get-tuple-element.30.pot_ref, f32[64,1024]{1,0:T(8,128)S(1)} %copy-done, f32[64,1024]{1,0:T(8,128)S(1)} %collective-permute-done.4.refs_1_, ...), custom_call_target="tpu_custom_call" | custom-call | tf_op jit(solution)/shard_map/ready/pallas_call | solution.py:534
  75.2 0.0 collective-permute-done.26
  75.2 6.2 %collective-permute-start.22 = (f32[2,8,128]{2,1,0:T(8,128)S(1)}, f32[2,8,128]{2,1,0:T(8,128)S(1)}, u32[]{:S(2)}, u32[]{:S(2)}) collective-permute-start(f32[2,8,128]{2,1,0:T(8,128)S(1)} %pad_maximum_fusion.1.refs_12_), channel_id=1, source_target_pairs={{0,2},{1,3},{2,0},{3,1},{4,6},{5,7},{6,4},{7,5},{8,10},{9,11},{10,... | collective-permute-start | bytes 24584 | tf_op jit(solution)/shard_map/ppermute | solution.py:399
  81.4 0.7 collective-permute-start.23
  82.1 0.0 collective-permute-done.10.refs_1_
  82.1 1.6 %collective-permute-start.24 = (f32[2,8,128]{2,1,0:T(8,128)S(1)}, f32[2,8,128]{2,1,0:T(8,128)S(1)}, u32[]{:S(2)}, u32[]{:S(2)}) collective-permute-start(f32[2,8,128]{2,1,0:T(8,128)S(1)} %pad_maximum_fusion.1.refs_12_), channel_id=1, source_target_pairs={{0,6},{1,7},{2,4},{3,5},{4,2},{5,3},{6,0},{7,1},{8,14},{9,15},{10,... | collective-permute-start | bytes 24584 | tf_op jit(solution)/shard_map/ppermute | solution.py:399
  83.7 0.8 add_divide_fusion
  84.5 1.3 %ready.7 = (f32[2048,512]{1,0:T(8,128)S(1)}, bf16[144,2048]{1,0:T(8,128)(2,1)S(1)}, f32[16,128]{1,0:T(8,128)S(1)}) custom-call(bf16[256,512]{1,0:T(8,128)(2,1)S(1)} %get-tuple-element.26.xop_ref, f32[32,128]{1,0:T(8,128)S(1)} %get-tuple-element.30.pot_ref, f32[64,1024]{1,0:T(8,128)S(1)} %collective-permute-done.9.refs_0_, ...), custom_call_target="tpu_custom_call" | custom-call | tf_op jit(solution)/shard_map/ready/pallas_call | solution.py:534
  85.8 1.2 %ready.6 = (f32[2048,512]{1,0:T(8,128)S(1)}, bf16[144,2048]{1,0:T(8,128)(2,1)S(1)}, f32[16,128]{1,0:T(8,128)S(1)}) custom-call(bf16[256,512]{1,0:T(8,128)(2,1)S(1)} %get-tuple-element.26.xop_ref, f32[32,128]{1,0:T(8,128)S(1)} %get-tuple-element.30.pot_ref, f32[64,1024]{1,0:T(8,128)S(1)} %collective-permute-done.7.refs_0_, ...), custom_call_target="tpu_custom_call" | custom-call | tf_op jit(solution)/shard_map/ready/pallas_call | solution.py:534
  87.1 0.0 collective-permute-done.6.refs_1_
  87.1 1.4 %ready.5 = (f32[2048,512]{1,0:T(8,128)S(1)}, bf16[144,2048]{1,0:T(8,128)(2,1)S(1)}, f32[16,128]{1,0:T(8,128)S(1)}) custom-call(bf16[256,512]{1,0:T(8,128)(2,1)S(1)} %get-tuple-element.26.xop_ref, f32[32,128]{1,0:T(8,128)S(1)} %get-tuple-element.30.pot_ref, f32[64,1024]{1,0:T(8,128)S(1)} %collective-permute-done.5.refs_0_, ...), custom_call_target="tpu_custom_call" | custom-call | tf_op jit(solution)/shard_map/ready/pallas_call | solution.py:534
  88.5 0.0 collective-permute-done.23.refs_14_
  88.5 0.0 collective-permute-done.24.refs_15_
  88.5 6.2 %final.1 = f32[64,512]{1,0:T(8,128)} custom-call(f32[2048,512]{1,0:T(8,128)S(1)} %get-tuple-element.31.refs_0_, f32[2048,512]{1,0:T(8,128)S(1)} %get-tuple-element.32.refs_1_, f32[2048,512]{1,0:T(8,128)S(1)} %get-tuple-element.33.refs_2_, f32[2048,512]{1,0:T(8,128)S(1)} %get-tuple-element.34.refs_3_, bf16[144,2048]{1,0:T(8,128)(2,1)S(1)} %get-tuple-element.35.refs_4_, ...), custom_call_target="tpu_custom_call" | custom-call | tf_op jit(solution)/shard_map/final/pallas_call | solution.py:553
  (12 shorter events, 0.1 us)
Async XLA Ops:
  6.4 1.4 %collective-permute-start = (f32[40,128]{1,0:T(8,128)S(1)}, f32[40,128]{1,0:T(8,128)S(1)}, u32[]{:S(2)}, u32[]{:S(2)}) collective-permute-start(f32[40,128]{1,0:T(8,128)S(1)} %get-tuple-element.29), channel_id=1, source_target_pairs={{0,1},{1,0},{2,3},{3,2},{4,5},{5,4},{6,7},{7,6},{8,9},{9,8},{10,11... | collective-permute-start | bytes 61448 | tf_op jit(solution)/shard_map/ppermute | solution.py:399
  7.8 5.6 %collective-permute-start.1 = (f32[48,128]{1,0:T(8,128)S(1)}, f32[48,128]{1,0:T(8,128)S(1)}, u32[]{:S(2)}, u32[]{:S(2)}) collective-permute-start(f32[48,128]{1,0:T(8,128)S(1)} %pad_maximum_fusion.refs_0_.refs_2_), channel_id=1, source_target_pairs={{0,2},{1,3},{2,0},{3,1},{4,6},{5,7},{6,4},{7,5},{8,10},{9,11},{10,... | collective-permute-start | bytes 73736 | tf_op jit(solution)/shard_map/ppermute | solution.py:399
  10.8 4.9 %collective-permute-start.2 = (f32[48,128]{1,0:T(8,128)S(1)}, f32[48,128]{1,0:T(8,128)S(1)}, u32[]{:S(2)}, u32[]{:S(2)}) collective-permute-start(f32[48,128]{1,0:T(8,128)S(1)} %pad_maximum_fusion.refs_0_.refs_2_), channel_id=1, source_target_pairs={{0,4},{1,5},{2,6},{3,7},{4,0},{5,1},{6,2},{7,3},{8,12},{9,13},{10,... | collective-permute-start | bytes 73736 | tf_op jit(solution)/shard_map/ppermute | solution.py:399
  13.4 5.6 %collective-permute-start.3 = (f32[48,128]{1,0:T(8,128)S(1)}, f32[48,128]{1,0:T(8,128)S(1)}, u32[]{:S(2)}, u32[]{:S(2)}) collective-permute-start(f32[48,128]{1,0:T(8,128)S(1)} %pad_maximum_fusion.refs_0_.refs_2_), channel_id=1, source_target_pairs={{0,6},{1,7},{2,4},{3,5},{4,2},{5,3},{6,0},{7,1},{8,14},{9,15},{10,... | collective-permute-start | bytes 73736 | tf_op jit(solution)/shard_map/ppermute | solution.py:399
  23.0 3.7 %collective-permute-start.11 = (f32[8,128]{1,0:T(8,128)S(1)}, f32[8,128]{1,0:T(8,128)S(1)}, u32[]{:S(2)}, u32[]{:S(2)}) collective-permute-start(f32[8,128]{1,0:T(8,128)S(1)} %get-tuple-element.43.refs_0_), channel_id=1, source_target_pairs={{0,8},{8,0},{16,24},{24,16},{1,9},{9,1},{17,25},{25,17},{2,10},{10... | collective-permute-start | bytes 12296 | tf_op jit(solution)/shard_map/ppermute | solution.py:399
  24.5 3.6 %collective-permute-start.12 = (f32[8,128]{1,0:T(8,128)S(1)}, f32[8,128]{1,0:T(8,128)S(1)}, u32[]{:S(2)}, u32[]{:S(2)}) collective-permute-start(f32[8,128]{1,0:T(8,128)S(1)} %get-tuple-element.43.refs_0_), channel_id=1, source_target_pairs={{0,16},{8,24},{16,0},{24,8},{1,17},{9,25},{17,1},{25,9},{2,18},{10... | collective-permute-start | bytes 12296 | tf_op jit(solution)/shard_map/ppermute | solution.py:399
  26.0 4.5 %collective-permute-start.13 = (f32[8,128]{1,0:T(8,128)S(1)}, f32[8,128]{1,0:T(8,128)S(1)}, u32[]{:S(2)}, u32[]{:S(2)}) collective-permute-start(f32[8,128]{1,0:T(8,128)S(1)} %get-tuple-element.43.refs_0_), channel_id=1, source_target_pairs={{0,24},{8,16},{16,8},{24,0},{1,25},{9,17},{17,9},{25,1},{2,26},{10... | collective-permute-start | bytes 12296 | tf_op jit(solution)/shard_map/ppermute | solution.py:399
  33.2 1.2 %collective-permute-start.14 = (f32[32,128]{1,0:T(8,128)S(1)}, f32[32,128]{1,0:T(8,128)S(1)}, u32[]{:S(2)}, u32[]{:S(2)}) collective-permute-start(f32[32,128]{1,0:T(8,128)S(1)} %get-tuple-element.47), channel_id=1, source_target_pairs={{0,1},{1,0},{2,3},{3,2},{4,5},{5,4},{6,7},{7,6},{8,9},{9,8},{10,11... | collective-permute-start | bytes 49160 | tf_op jit(solution)/shard_map/ppermute | solution.py:399
  34.4 5.9 %collective-permute-start.15 = (f32[32,128]{1,0:T(8,128)S(1)}, f32[32,128]{1,0:T(8,128)S(1)}, u32[]{:S(2)}, u32[]{:S(2)}) collective-permute-start(f32[32,128]{1,0:T(8,128)S(1)} %add.30.refs_0_), channel_id=1, source_target_pairs={{0,2},{1,3},{2,0},{3,1},{4,6},{5,7},{6,4},{7,5},{8,10},{9,11},{10,... | collective-permute-start | bytes 49160 | tf_op jit(solution)/shard_map/ppermute | solution.py:399
  34.4 5.9 %collective-permute-start.16 = (f32[32,128]{1,0:T(8,128)S(1)}, f32[32,128]{1,0:T(8,128)S(1)}, u32[]{:S(2)}, u32[]{:S(2)}) collective-permute-start(f32[32,128]{1,0:T(8,128)S(1)} %add.30.refs_0_), channel_id=1, source_target_pairs={{0,4},{1,5},{2,6},{3,7},{4,0},{5,1},{6,2},{7,3},{8,12},{9,13},{10,... | collective-permute-start | bytes 49160 | tf_op jit(solution)/shard_map/ppermute | solution.py:399
  35.3 5.5 %collective-permute-start.17 = (f32[32,128]{1,0:T(8,128)S(1)}, f32[32,128]{1,0:T(8,128)S(1)}, u32[]{:S(2)}, u32[]{:S(2)}) collective-permute-start(f32[32,128]{1,0:T(8,128)S(1)} %add.30.refs_0_), channel_id=1, source_target_pairs={{0,6},{1,7},{2,4},{3,5},{4,2},{5,3},{6,0},{7,1},{8,14},{9,15},{10,... | collective-permute-start | bytes 49160 | tf_op jit(solution)/shard_map/ppermute | solution.py:399
  40.8 9.4 %copy-start = (f32[64,1024]{1,0:T(8,128)S(1)}, f32[64,1024]{1,0:T(8,128)}, u32[]{:S(2)}) copy-start(f32[64,1024]{1,0:T(8,128)} %refs_0_.1) | copy-start | bytes 786436
  46.6 7.1 %collective-permute-start.18 = (f32[8,128]{1,0:T(8,128)S(1)}, f32[8,128]{1,0:T(8,128)S(1)}, u32[]{:S(2)}, u32[]{:S(2)}) collective-permute-start(f32[8,128]{1,0:T(8,128)S(1)} %get-tuple-element.48), channel_id=1, source_target_pairs={{0,8},{8,0},{16,24},{24,16},{1,9},{9,1},{17,25},{25,17},{2,10},{10... | collective-permute-start | bytes 12296 | tf_op jit(solution)/shard_map/ppermute | solution.py:399
  47.2 7.4 %collective-permute-start.19 = (f32[8,128]{1,0:T(8,128)S(1)}, f32[8,128]{1,0:T(8,128)S(1)}, u32[]{:S(2)}, u32[]{:S(2)}) collective-permute-start(f32[8,128]{1,0:T(8,128)S(1)} %get-tuple-element.48), channel_id=1, source_target_pairs={{0,16},{8,24},{16,0},{24,8},{1,17},{9,25},{17,1},{25,9},{2,18},{10... | collective-permute-start | bytes 12296 | tf_op jit(solution)/shard_map/ppermute | solution.py:399
  47.7 6.9 %collective-permute-start.20 = (f32[8,128]{1,0:T(8,128)S(1)}, f32[8,128]{1,0:T(8,128)S(1)}, u32[]{:S(2)}, u32[]{:S(2)}) collective-permute-start(f32[8,128]{1,0:T(8,128)S(1)} %get-tuple-element.48), channel_id=1, source_target_pairs={{0,24},{8,16},{16,8},{24,0},{1,25},{9,17},{17,9},{25,1},{2,26},{10... | collective-permute-start | bytes 12296 | tf_op jit(solution)/shard_map/ppermute | solution.py:399
  50.2 11.0 %collective-permute-start.9 = (f32[64,1024]{1,0:T(8,128)S(1)}, f32[64,1024]{1,0:T(8,128)S(1)}, u32[]{:S(2)}, u32[]{:S(2)}) collective-permute-start(f32[64,1024]{1,0:T(8,128)S(1)} %copy-done), channel_id=1, source_target_pairs={{0,6},{1,7},{2,4},{3,5},{4,2},{5,3},{6,0},{7,1},{8,14},{9,15},{10,... | collective-permute-start | bytes 786440 | tf_op jit(solution)/shard_map/ppermute | solution.py:399
  53.7 19.1 %collective-permute-start.7 = (f32[64,1024]{1,0:T(8,128)S(1)}, f32[64,1024]{1,0:T(8,128)S(1)}, u32[]{:S(2)}, u32[]{:S(2)}) collective-permute-start(f32[64,1024]{1,0:T(8,128)S(1)} %copy-done), channel_id=1, source_target_pairs={{0,4},{1,5},{2,6},{3,7},{4,0},{5,1},{6,2},{7,3},{8,12},{9,13},{10,... | collective-permute-start | bytes 786440 | tf_op jit(solution)/shard_map/ppermute | solution.py:399
  53.7 19.6 %collective-permute-start.5 = (f32[64,1024]{1,0:T(8,128)S(1)}, f32[64,1024]{1,0:T(8,128)S(1)}, u32[]{:S(2)}, u32[]{:S(2)}) collective-permute-start(f32[64,1024]{1,0:T(8,128)S(1)} %copy-done), channel_id=1, source_target_pairs={{0,2},{1,3},{2,0},{3,1},{4,6},{5,7},{6,4},{7,5},{8,10},{9,11},{10,... | collective-permute-start | bytes 786440 | tf_op jit(solution)/shard_map/ppermute | solution.py:399
  54.6 1.2 %collective-permute-start.21 = (f32[8,128]{1,0:T(8,128)S(1)}, f32[8,128]{1,0:T(8,128)S(1)}, u32[]{:S(2)}, u32[]{:S(2)}) collective-permute-start(f32[8,128]{1,0:T(8,128)S(1)} %get-tuple-element.50), channel_id=1, source_target_pairs={{0,1},{1,0},{2,3},{3,2},{4,5},{5,4},{6,7},{7,6},{8,9},{9,8},{10,11... | collective-permute-start | bytes 12296 | tf_op jit(solution)/shard_map/ppermute | solution.py:399
  54.7 18.7 %collective-permute-start.4 = (f32[64,1024]{1,0:T(8,128)S(1)}, f32[64,1024]{1,0:T(8,128)S(1)}, u32[]{:S(2)}, u32[]{:S(2)}) collective-permute-start(f32[64,1024]{1,0:T(8,128)S(1)} %copy-done), channel_id=1, source_target_pairs={{0,1},{1,0},{2,3},{3,2},{4,5},{5,4},{6,7},{7,6},{8,9},{9,8},{10,11... | collective-permute-start | bytes 786440 | tf_op jit(solution)/shard_map/ppermute | solution.py:399
  55.8 18.0 %collective-permute-start.25 = (f32[64,1024]{1,0:T(8,128)S(1)}, f32[64,1024]{1,0:T(8,128)S(1)}, u32[]{:S(2)}, u32[]{:S(2)}) collective-permute-start(f32[64,1024]{1,0:T(8,128)S(1)} %get-tuple-element.49), channel_id=1, source_target_pairs={{0,8},{8,0},{16,24},{24,16},{1,9},{9,1},{17,25},{25,17},{2,10},{10... | collective-permute-start | bytes 786440 | tf_op jit(solution)/shard_map/ppermute | solution.py:399
  61.2 14.0 %collective-permute-start.26 = (f32[64,1024]{1,0:T(8,128)S(1)}, f32[64,1024]{1,0:T(8,128)S(1)}, u32[]{:S(2)}, u32[]{:S(2)}) collective-permute-start(f32[64,1024]{1,0:T(8,128)S(1)} %get-tuple-element.49), channel_id=1, source_target_pairs={{0,16},{8,24},{16,0},{24,8},{1,17},{9,25},{17,1},{25,9},{2,18},{10... | collective-permute-start | bytes 786440 | tf_op jit(solution)/shard_map/ppermute | solution.py:399
  72.9 8.5 %collective-permute-start.27 = (f32[64,1024]{1,0:T(8,128)S(1)}, f32[64,1024]{1,0:T(8,128)S(1)}, u32[]{:S(2)}, u32[]{:S(2)}) collective-permute-start(f32[64,1024]{1,0:T(8,128)S(1)} %get-tuple-element.49), channel_id=1, source_target_pairs={{0,24},{8,16},{16,8},{24,0},{1,25},{9,17},{17,9},{25,1},{2,26},{10... | collective-permute-start | bytes 786440 | tf_op jit(solution)/shard_map/ppermute | solution.py:399
  73.3 8.8 %collective-permute-start.10 = (f32[64,1024]{1,0:T(8,128)S(1)}, f32[64,1024]{1,0:T(8,128)S(1)}, u32[]{:S(2)}, u32[]{:S(2)}) collective-permute-start(f32[64,1024]{1,0:T(8,128)S(1)} %collective-permute-done.9.refs_0_), channel_id=1, source_target_pairs={{0,1},{1,0},{2,3},{3,2},{4,5},{5,4},{6,7},{7,6},{8,9},{9,8},{10,11... | collective-permute-start | bytes 786440 | tf_op jit(solution)/shard_map/ppermute | solution.py:399
  73.4 12.4 %collective-permute-start.8 = (f32[64,1024]{1,0:T(8,128)S(1)}, f32[64,1024]{1,0:T(8,128)S(1)}, u32[]{:S(2)}, u32[]{:S(2)}) collective-permute-start(f32[64,1024]{1,0:T(8,128)S(1)} %collective-permute-done.7.refs_0_), channel_id=1, source_target_pairs={{0,1},{1,0},{2,3},{3,2},{4,5},{5,4},{6,7},{7,6},{8,9},{9,8},{10,11... | collective-permute-start | bytes 786440 | tf_op jit(solution)/shard_map/ppermute | solution.py:399
  73.9 13.2 %collective-permute-start.6 = (f32[64,1024]{1,0:T(8,128)S(1)}, f32[64,1024]{1,0:T(8,128)S(1)}, u32[]{:S(2)}, u32[]{:S(2)}) collective-permute-start(f32[64,1024]{1,0:T(8,128)S(1)} %collective-permute-done.5.refs_0_), channel_id=1, source_target_pairs={{0,1},{1,0},{2,3},{3,2},{4,5},{5,4},{6,7},{7,6},{8,9},{9,8},{10,11... | collective-permute-start | bytes 786440 | tf_op jit(solution)/shard_map/ppermute | solution.py:399
  75.2 13.3 %collective-permute-start.22 = (f32[2,8,128]{2,1,0:T(8,128)S(1)}, f32[2,8,128]{2,1,0:T(8,128)S(1)}, u32[]{:S(2)}, u32[]{:S(2)}) collective-permute-start(f32[2,8,128]{2,1,0:T(8,128)S(1)} %pad_maximum_fusion.1.refs_12_), channel_id=1, source_target_pairs={{0,2},{1,3},{2,0},{3,1},{4,6},{5,7},{6,4},{7,5},{8,10},{9,11},{10,... | collective-permute-start | bytes 24584 | tf_op jit(solution)/shard_map/ppermute | solution.py:399
  81.4 7.1 %collective-permute-start.23 = (f32[2,8,128]{2,1,0:T(8,128)S(1)}, f32[2,8,128]{2,1,0:T(8,128)S(1)}, u32[]{:S(2)}, u32[]{:S(2)}) collective-permute-start(f32[2,8,128]{2,1,0:T(8,128)S(1)} %pad_maximum_fusion.1.refs_12_), channel_id=1, source_target_pairs={{0,4},{1,5},{2,6},{3,7},{4,0},{5,1},{6,2},{7,3},{8,12},{9,13},{10,... | collective-permute-start | bytes 24584 | tf_op jit(solution)/shard_map/ppermute | solution.py:399
  82.1 6.4 %collective-permute-start.24 = (f32[2,8,128]{2,1,0:T(8,128)S(1)}, f32[2,8,128]{2,1,0:T(8,128)S(1)}, u32[]{:S(2)}, u32[]{:S(2)}) collective-permute-start(f32[2,8,128]{2,1,0:T(8,128)S(1)} %pad_maximum_fusion.1.refs_12_), channel_id=1, source_target_pairs={{0,6},{1,7},{2,4},{3,5},{4,2},{5,3},{6,0},{7,1},{8,14},{9,15},{10,... | collective-permute-start | bytes 24584 | tf_op jit(solution)/shard_map/ppermute | solution.py:399
